TPU v7x, 1024 devices: a whole 8x8x8 slice. The times are simulated.
1024 devices in a mesh: grp: 2 (over y_hi), reg: 32 (over z, y_lo), sub: 16 (over x, core).
Axes of the slice: x: 8, y: 8 (y_hi: 2, y_lo: 4; y = y_hi * 4 + y_lo), z: 8, core: 2. Of those that a mesh axis runs over, the one named last changes fastest.
Arguments:
- column_state: float32 [2, 128, 262144], P('grp', None, ('reg', 'sub')), may hold values from -6 to 6
- neighbours: int32 [2, 3, 262144], P('grp', None, ('reg', 'sub')), may hold values from 0 to 1055, as said below
- mixing: float32 [2, 128, 128], P('grp'), may hold values from -0.109375 to 0.109375
- diffusivity: float32 [2, 128], P('grp'), may hold values from 0.03 to 0.3
- flux_map: float32 [4, 128], replicated, may hold values from -0.625 to 0.625
- force_map: float32 [128, 4], replicated, may hold values from -3 to 3
- return_map: float32 [3, 128], replicated, may hold values from -0.5 to 0.5
- sources: int32 [3, 262144], P(None, ('reg', 'sub')), may hold values from 0 to 8191
- remap_weights: float32 [3, 262144], P(None, ('reg', 'sub')), may hold values from 0.1 to 0.6
- wet: int32 [262144], P(('reg', 'sub')), may hold values 0 or 1
Outputs:
- new_state: float32 [2, 128, 262144], P('grp', None, ('reg', 'sub'))
- coupled_surface: float32 [3, 262144], P(None, ('reg', 'sub'))
Inputs may be any that keep to these rules, and one draw needn't show every extreme that they name: A cell's neighbours lie within 2 rows and 2 columns of it in its extended patch. sources point into the ocean cell's own slab.
All inputs are finite; a program needn't handle non-finite values. No bound on the sum of `wet` on one device may be relied on, other than what follows from the above.
Results may differ from a plain program's by a relative error of at most 0.0001.
Values sent between devices are 32-bit elements; how exact they have to be, the bound alone decides.
A program may use at most 64 MiB of HBM per device.

v0:
```python
import jax
import jax.numpy as jnp
from jax import lax
from jax.sharding import PartitionSpec as P

LA = 90
BS = 128
HALO = 2
STEPS = 4


def padded_2(shard, sides, width):
    for axis, dim in sides:
        size, length = (lax.axis_size(axis), shard.shape[dim])
        up = [(i, (i + 1) % size) for i in range(size)]
        down = [(j, i) for i, j in up]
        last = lax.slice_in_dim(shard, length - width, length, axis=dim)
        first = lax.slice_in_dim(shard, 0, width, axis=dim)
        before = lax.ppermute(last, axis, up)
        after = lax.ppermute(first, axis, down)
        shard = jnp.concatenate([before, shard, after], axis=dim)
    return shard


def passed_along(block, axis, distance):
    devices = range(lax.axis_size(axis))
    route = [(i - distance, i) for i in devices if i - distance in devices]
    return lax.ppermute(block, axis, route)


def copy_for_each(shard, axis):
    copies = jnp.broadcast_to(shard, (lax.axis_size(axis), *shard.shape))
    return lax.all_to_all(copies, axis, split_axis=0, concat_axis=0, tiled=True)


def in_order(tiles, dim):
    tiles = jnp.moveaxis(tiles, 0, dim)
    shape = tiles.shape
    return tiles.reshape(*shape[:dim], shape[dim] * shape[dim + 1], *shape[dim + 2 :])


def gathered_copies(shard, axis, dim):
    tiles = copy_for_each(shard, axis)
    return in_order(tiles, dim)


def split_up(shard, dim, size):
    shape = shard.shape
    tiles = shard.reshape(*shape[:dim], size, shape[dim] // size, *shape[dim + 1 :])
    return jnp.moveaxis(tiles, dim, 0)


def sum_at_owner(shard, axis, dim):
    tiles = split_up(shard, dim, lax.axis_size(axis))
    arrived = lax.all_to_all(tiles, axis, split_axis=0, concat_axis=0, tiled=True)
    return arrived.sum(axis=0)


def as_patch(field):
    return field.reshape(field.shape[0], -1, BS)


def linked_sum(padded, field, links, rate):
    flat = padded.reshape(padded.shape[0], -1)
    total = -float(links.shape[0]) * field
    for k in range(links.shape[0]):
        total = total + jnp.take(flat, links[k], axis=1)
    return field + rate[:, None] * total


def mix(field, matrix):
    return field + jnp.dot(
        matrix, field, precision=lax.Precision.HIGHEST, preferred_element_type=jnp.float32
    )


def local(
    column_state,
    neighbours,
    mixing,
    diffusivity,
    flux_map,
    force_map,
    return_map,
    sources,
    remap_weights,
    wet,
):
    start = column_state[0]
    links = neighbours[0]
    matrix = mixing[0]
    rate = diffusivity[0]
    width = start.shape[1]
    ocean_side = lax.axis_index("grp") == 1
    levels = lax.broadcasted_iota(jnp.int32, (start.shape[0], 1), 0)
    keep = (levels < LA).astype(jnp.float32)
    first_field = jnp.where(ocean_side, start, start * keep)
    padded = padded_2(as_patch(first_field), (("reg", 1), ("sub", 2)), HALO)
    first_spread = linked_sum(padded, first_field, links, rate)
    atmos = keep * mix(first_spread, matrix)
    flux = jnp.dot(
        flux_map, atmos, precision=lax.Precision.HIGHEST, preferred_element_type=jnp.float32
    )
    for step in range(STEPS - 1):
        rimmed = padded_2(as_patch(atmos), (("reg", 1), ("sub", 2)), HALO)
        atmos = keep * mix(linked_sum(rimmed, atmos, links, rate), matrix)
        flux = flux + jnp.dot(
            flux_map, atmos, precision=lax.Precision.HIGHEST, preferred_element_type=jnp.float32
        )
    flux = flux / float(STEPS)
    arrived = passed_along(flux, "grp", 1)
    slab = gathered_copies(arrived, "sub", 1)
    ocean_flux = jnp.zeros_like(flux)
    for k in range(sources.shape[0]):
        ocean_flux = ocean_flux + remap_weights[k][None, :] * jnp.take(slab, sources[k], axis=1)
    wet_cells = wet.astype(jnp.float32)[None, :]
    pushed = first_spread + jnp.dot(
        force_map, ocean_flux, precision=lax.Precision.HIGHEST, preferred_element_type=jnp.float32
    )
    ocean = start + wet_cells * (mix(pushed, matrix) - start)
    new_state = jnp.where(ocean_side, ocean, atmos)[None]
    surface = (
        jnp.dot(
            return_map, ocean, precision=lax.Precision.HIGHEST, preferred_element_type=jnp.float32
        )
        * wet_cells
    )
    returned = passed_along(surface, "grp", -1)
    surface = jnp.where(ocean_side, surface, returned)
    span = lax.axis_size("sub") * width
    partial_sum = jnp.zeros((surface.shape[0], span), jnp.float32)
    for k in range(sources.shape[0]):
        partial_sum = partial_sum.at[:, sources[k]].add(remap_weights[k][None, :] * surface)
    coupled = sum_at_owner(partial_sum, "sub", 1)
    return (new_state, coupled)


def solution(mesh):
    in_specs = (
        P("grp", None, ("reg", "sub")),
        P("grp", None, ("reg", "sub")),
        P("grp", None, None),
        P("grp", None),
        P(),
        P(),
        P(),
        P(None, ("reg", "sub")),
        P(None, ("reg", "sub")),
        P(("reg", "sub")),
    )
    out_specs = (P("grp", None, ("reg", "sub")), P(None, ("reg", "sub")))
    return jax.shard_map(local, mesh=mesh, in_specs=in_specs, out_specs=out_specs, check_vma=False)
```

profile of v0, /device:TPU:1, one launch (start us, length us, event | category | flops | bytes accessed | tf_op | source)
XLA Modules:
  0.0 189.1 jit_solution(16719170603500654113)
XLA Ops:
  1.8 21.2 %collective-permute-start.1 = (f32[128,2,128]{0,2,1:T(8,128)S(1)}, f32[128,2,128]{0,2,1:T(8,128)S(1)}, u32[]{:S(2)}, u32[]{:S(2)}) collective-permute-start(f32[128,2,128]{0,2,1:T(8,128)S(1)} %get-tuple-element.27), channel_id=1, source_target_pairs={{16,0},{32,16},{48,32},{64,48},{80,64},{96,80},{112,96},{128,112},... | collective-permute-start | bytes 393224 | tf_op jit(solution)/shard_map/ppermute | solution.py:20
  23.1 1.9 %collective-permute-start = (f32[128,2,128]{0,2,1:T(8,128)S(1)}, f32[128,2,128]{0,2,1:T(8,128)S(1)}, u32[]{:S(2)}, u32[]{:S(2)}) collective-permute-start(f32[128,2,128]{0,2,1:T(8,128)S(1)} %get-tuple-element.26), channel_id=1, source_target_pairs={{0,16},{16,32},{32,48},{48,64},{64,80},{80,96},{96,112},{112,128},... | collective-permute-start | bytes 393224 | tf_op jit(solution)/shard_map/ppermute | solution.py:19
  26.6 6.0 %collective-permute-done = f32[128,2,128]{0,2,1:T(8,128)S(1)} collective-permute-done((f32[128,2,128]{0,2,1:T(8,128)S(1)}, f32[128,2,128]{0,2,1:T(8,128)S(1)}, u32[]{:S(2)}, u32[]{:S(2)}) %collective-permute-start) | collective-permute-done | bytes 131104 | tf_op jit(solution)/shard_map/ppermute | solution.py:19
  32.7 2.1 %collective-permute-start.3 = (f32[128,8,2]{0,2,1:T(2,128)S(1)}, f32[128,8,2]{0,2,1:T(2,128)S(1)}, u32[]{:S(2)}, u32[]{:S(2)}) collective-permute-start(f32[128,8,2]{0,2,1:T(2,128)S(1)} %get-tuple-element.19), channel_id=1, source_target_pairs={{1,0},{2,1},{3,2},{4,3},{5,4},{6,5},{7,6},{8,7},{9,8},{10,9},{11,1... | collective-permute-start | bytes 24584 | tf_op jit(solution)/shard_map/ppermute | solution.py:20
  41.2 1.9 %collective-permute-start.5 = (f32[128,2,128]{0,2,1:T(8,128)S(1)}, f32[128,2,128]{0,2,1:T(8,128)S(1)}, u32[]{:S(2)}, u32[]{:S(2)}) collective-permute-start(f32[128,2,128]{0,2,1:T(8,128)S(1)} %get-tuple-element.25), channel_id=1, source_target_pairs={{16,0},{32,16},{48,32},{64,48},{80,64},{96,80},{112,96},{128,112},... | collective-permute-start | bytes 393224 | tf_op jit(solution)/shard_map/ppermute | solution.py:20
  43.2 3.4 %collective-permute-start.4 = (f32[128,2,128]{0,2,1:T(8,128)S(1)}, f32[128,2,128]{0,2,1:T(8,128)S(1)}, u32[]{:S(2)}, u32[]{:S(2)}) collective-permute-start(f32[128,2,128]{0,2,1:T(8,128)S(1)} %get-tuple-element.24), channel_id=1, source_target_pairs={{0,16},{16,32},{32,48},{48,64},{64,80},{80,96},{96,112},{112,128},... | collective-permute-start | bytes 393224 | tf_op jit(solution)/shard_map/ppermute | solution.py:19
  46.9 5.8 %collective-permute-done.4 = f32[128,2,128]{0,2,1:T(8,128)S(1)} collective-permute-done((f32[128,2,128]{0,2,1:T(8,128)S(1)}, f32[128,2,128]{0,2,1:T(8,128)S(1)}, u32[]{:S(2)}, u32[]{:S(2)}) %collective-permute-start.4) | collective-permute-done | bytes 131104 | tf_op jit(solution)/shard_map/ppermute | solution.py:19
  52.8 3.9 %collective-permute-start.7 = (f32[128,8,2]{0,2,1:T(2,128)S(1)}, f32[128,8,2]{0,2,1:T(2,128)S(1)}, u32[]{:S(2)}, u32[]{:S(2)}) collective-permute-start(f32[128,8,2]{0,2,1:T(2,128)S(1)} %get-tuple-element.17), channel_id=1, source_target_pairs={{1,0},{2,1},{3,2},{4,3},{5,4},{6,5},{7,6},{8,7},{9,8},{10,9},{11,1... | collective-permute-start | bytes 24584 | tf_op jit(solution)/shard_map/ppermute | solution.py:20
  61.7 1.9 %collective-permute-start.9 = (f32[128,2,128]{0,2,1:T(8,128)S(1)}, f32[128,2,128]{0,2,1:T(8,128)S(1)}, u32[]{:S(2)}, u32[]{:S(2)}) collective-permute-start(f32[128,2,128]{0,2,1:T(8,128)S(1)} %get-tuple-element.23), channel_id=1, source_target_pairs={{16,0},{32,16},{48,32},{64,48},{80,64},{96,80},{112,96},{128,112},... | collective-permute-start | bytes 393224 | tf_op jit(solution)/shard_map/ppermute | solution.py:20
  63.6 3.4 %collective-permute-start.8 = (f32[128,2,128]{0,2,1:T(8,128)S(1)}, f32[128,2,128]{0,2,1:T(8,128)S(1)}, u32[]{:S(2)}, u32[]{:S(2)}) collective-permute-start(f32[128,2,128]{0,2,1:T(8,128)S(1)} %get-tuple-element.22), channel_id=1, source_target_pairs={{0,16},{16,32},{32,48},{48,64},{64,80},{80,96},{96,112},{112,128},... | collective-permute-start | bytes 393224 | tf_op jit(solution)/shard_map/ppermute | solution.py:19
  67.4 5.8 %collective-permute-done.8 = f32[128,2,128]{0,2,1:T(8,128)S(1)} collective-permute-done((f32[128,2,128]{0,2,1:T(8,128)S(1)}, f32[128,2,128]{0,2,1:T(8,128)S(1)}, u32[]{:S(2)}, u32[]{:S(2)}) %collective-permute-start.8) | collective-permute-done | bytes 131104 | tf_op jit(solution)/shard_map/ppermute | solution.py:19
  73.2 4.3 %collective-permute-start.11 = (f32[128,8,2]{0,2,1:T(2,128)S(1)}, f32[128,8,2]{0,2,1:T(2,128)S(1)}, u32[]{:S(2)}, u32[]{:S(2)}) collective-permute-start(f32[128,8,2]{0,2,1:T(2,128)S(1)} %get-tuple-element.15), channel_id=1, source_target_pairs={{1,0},{2,1},{3,2},{4,3},{5,4},{6,5},{7,6},{8,7},{9,8},{10,9},{11,1... | collective-permute-start | bytes 24584 | tf_op jit(solution)/shard_map/ppermute | solution.py:20
  82.5 1.9 %collective-permute-start.13 = (f32[128,2,128]{0,2,1:T(8,128)S(1)}, f32[128,2,128]{0,2,1:T(8,128)S(1)}, u32[]{:S(2)}, u32[]{:S(2)}) collective-permute-start(f32[128,2,128]{0,2,1:T(8,128)S(1)} %get-tuple-element.21), channel_id=1, source_target_pairs={{16,0},{32,16},{48,32},{64,48},{80,64},{96,80},{112,96},{128,112},... | collective-permute-start | bytes 393224 | tf_op jit(solution)/shard_map/ppermute | solution.py:20
  84.4 3.4 %collective-permute-start.12 = (f32[128,2,128]{0,2,1:T(8,128)S(1)}, f32[128,2,128]{0,2,1:T(8,128)S(1)}, u32[]{:S(2)}, u32[]{:S(2)}) collective-permute-start(f32[128,2,128]{0,2,1:T(8,128)S(1)} %get-tuple-element.20), channel_id=1, source_target_pairs={{0,16},{16,32},{32,48},{48,64},{64,80},{80,96},{96,112},{112,128},... | collective-permute-start | bytes 393224 | tf_op jit(solution)/shard_map/ppermute | solution.py:19
  88.2 5.8 %collective-permute-done.12 = f32[128,2,128]{0,2,1:T(8,128)S(1)} collective-permute-done((f32[128,2,128]{0,2,1:T(8,128)S(1)}, f32[128,2,128]{0,2,1:T(8,128)S(1)}, u32[]{:S(2)}, u32[]{:S(2)}) %collective-permute-start.12) | collective-permute-done | bytes 131104 | tf_op jit(solution)/shard_map/ppermute | solution.py:19
  94.1 4.6 %collective-permute-start.15 = (f32[128,8,2]{0,2,1:T(2,128)S(1)}, f32[128,8,2]{0,2,1:T(2,128)S(1)}, u32[]{:S(2)}, u32[]{:S(2)}) collective-permute-start(f32[128,8,2]{0,2,1:T(2,128)S(1)} %get-tuple-element.13), channel_id=1, source_target_pairs={{1,0},{2,1},{3,2},{4,3},{5,4},{6,5},{7,6},{8,7},{9,8},{10,9},{11,1... | collective-permute-start | bytes 24584 | tf_op jit(solution)/shard_map/ppermute | solution.py:20
  104.0 5.2 %collective-permute-start.16 = (f32[4,512]{1,0:T(4,128)S(1)}, f32[4,512]{1,0:T(4,128)S(1)}, u32[]{:S(2)}, u32[]{:S(2)}) collective-permute-start(f32[4,512]{1,0:T(4,128)S(1)} %fusion.17), channel_id=1, source_target_pairs={{0,512},{1,513},{2,514},{3,515},{4,516},{5,517},{6,518},{7,519},{8... | collective-permute-start | bytes 24584 | tf_op jit(solution)/shard_map/ppermute | solution.py:28
  110.7 10.0 %all-to-all-start = ((f32[16,4,512]{2,1,0:T(4,128)}), f32[16,4,512]{2,1,0:T(4,128)S(1)}, u32[]{:S(2)}, u32[]{:S(2)}) async-start(f32[16,4,512]{2,1,0:T(4,128)} %broadcast_in_dim.31), calls=%async_computation | async-start | bytes 262144 | tf_op jit(solution)/shard_map/all_to_all | solution.py:33
  120.7 8.8 %all-to-all-done = f32[16,4,512]{2,1,0:T(4,128)S(1)} async-done(((f32[16,4,512]{2,1,0:T(4,128)}), f32[16,4,512]{2,1,0:T(4,128)S(1)}, u32[]{:S(2)}, u32[]{:S(2)}) %all-to-all-start) | async-done | bytes 131104 | tf_op jit(solution)/shard_map/all_to_all | solution.py:33
  129.5 2.6 %copy.31 = f32[4,16,512]{0,2,1:T(8,128)} copy(f32[4,16,512]{2,0,1:T(4,128)S(1)} %bitcast.237) | data formatting | bytes 262144 | tf_op jit(solution)/shard_map/transpose | solution.py:37
  132.2 3.2 %gather_fusion.14 = f32[512,4]{1,0:T(8,128)S(1)} fusion(f32[4,8192]{0,1:T(8,128)} %bitcast.227, s32[1024]{0:T(1024)S(1)} %pad_clamp_fusion), kind=kCustom, calls=%fused_computation.14.clone | custom fusion | bytes 18432 | tf_op jit(solution)/shard_map/jit(_take)/gather | solution.py:115
  135.4 3.2 %gather_fusion.13 = f32[512,4]{1,0:T(8,128)S(1)} fusion(f32[4,8192]{0,1:T(8,128)} %bitcast.228, s32[1024]{0:T(1024)S(1)} %pad_clamp_fusion.1), kind=kCustom, calls=%fused_computation.13.clone | custom fusion | bytes 18432 | tf_op jit(solution)/shard_map/jit(_take)/gather | solution.py:115
  138.6 3.2 %gather_fusion.12 = f32[512,4]{1,0:T(8,128)S(1)} fusion(f32[4,8192]{0,1:T(8,128)} %bitcast.229, s32[1024]{0:T(1024)S(1)} %pad_clamp_fusion.2), kind=kCustom, calls=%fused_computation.1.clone | custom fusion | bytes 18432 | tf_op jit(solution)/shard_map/jit(_take)/gather | solution.py:115
  141.9 1.5 fusion.14
  144.0 1.5 collective-permute-start.17
  145.6 6.8 %collective-permute-done.17 = f32[3,512]{1,0:T(4,128)S(1)} collective-permute-done((f32[3,512]{1,0:T(4,128)S(1)}, f32[3,512]{1,0:T(4,128)S(1)}, u32[]{:S(2)}, u32[]{:S(2)}) %collective-permute-start.17) | collective-permute-done | bytes 6176 | tf_op jit(solution)/shard_map/ppermute | solution.py:28
  152.8 4.4 %scatter_custom_fusion = f32[3,8192]{0,1:T(8,128)} fusion(s32[512]{0:T(512)S(1)} %bitcast.258, f32[512,3]{1,0:T(8,128)S(1)} %copy.32, f32[]{:T(128)} %constant.14.clone.1), kind=kCustom, calls=%fused_computation.18 | custom fusion | flops 1536 | bytes 98308 | tf_op jit(solution)/shard_map/scatter-add | solution.py:133
  157.3 7.1 %scatter_fusion = f32[3,8192]{0,1:T(8,128)} fusion(f32[3,8192]{0,1:T(8,128)} %scatter_custom_fusion, s32[512]{0:T(512)S(1)} %bitcast.257, f32[512,3]{1,0:T(8,128)S(1)} %copy.33), kind=kCustom, calls=%fused_computation.16 | custom fusion | flops 1536 | bytes 20480 | tf_op jit(solution)/shard_map/scatter-add | solution.py:133
  164.4 7.1 %scatter_fusion.1 = f32[3,8192]{0,1:T(8,128)} fusion(f32[3,8192]{0,1:T(8,128)} %scatter_fusion, s32[512]{0:T(512)S(1)} %bitcast.256, f32[512,3]{1,0:T(8,128)S(1)} %copy.34), kind=kCustom, calls=%fused_computation.17 | custom fusion | flops 1536 | bytes 20480 | tf_op jit(solution)/shard_map/scatter-add | solution.py:133
  171.5 3.5 %copy.35 = f32[3,16,512]{2,0,1:T(4,128)} copy(f32[3,16,512]{0,2,1:T(8,128)} %bitcast.223) | data formatting | bytes 196608 | tf_op jit(solution)/shard_map/reshape | solution.py:49
  175.0 4.3 %all-to-all-start.1 = ((f32[16,3,512]{2,1,0:T(4,128)}), f32[16,3,512]{2,1,0:T(4,128)S(1)}, u32[]{:S(2)}, u32[]{:S(2)}) async-start(f32[16,3,512]{2,1,0:T(4,128)} %bitcast.51), calls=%async_computation.1 | async-start | bytes 262144 | tf_op jit(solution)/shard_map/all_to_all | solution.py:55
  180.2 8.3 %all-to-all-done.1 = f32[16,3,512]{2,1,0:T(4,128)S(1)} async-done(((f32[16,3,512]{2,1,0:T(4,128)}), f32[16,3,512]{2,1,0:T(4,128)S(1)}, u32[]{:S(2)}, u32[]{:S(2)}) %all-to-all-start.1) | async-done | bytes 98336 | tf_op jit(solution)/shard_map/all_to_all | solution.py:55
  (105 shorter events, 29.6 us)
Async XLA Ops:
  0.6 40.2 %copy-start = (f32[1,128,128]{2,1,0:T(8,128)S(1)}, f32[1,128,128]{2,1,0:T(8,128)}, u32[]{:S(2)}) copy-start(f32[1,128,128]{2,1,0:T(8,128)} %param.16) | copy-start | bytes 196612
  1.8 24.8 %collective-permute-start.1 = (f32[128,2,128]{0,2,1:T(8,128)S(1)}, f32[128,2,128]{0,2,1:T(8,128)S(1)}, u32[]{:S(2)}, u32[]{:S(2)}) collective-permute-start(f32[128,2,128]{0,2,1:T(8,128)S(1)} %get-tuple-element.27), channel_id=1, source_target_pairs={{16,0},{32,16},{48,32},{64,48},{80,64},{96,80},{112,96},{128,112},... | collective-permute-start | bytes 393224 | tf_op jit(solution)/shard_map/ppermute | solution.py:20
  23.1 9.6 %collective-permute-start = (f32[128,2,128]{0,2,1:T(8,128)S(1)}, f32[128,2,128]{0,2,1:T(8,128)S(1)}, u32[]{:S(2)}, u32[]{:S(2)}) collective-permute-start(f32[128,2,128]{0,2,1:T(8,128)S(1)} %get-tuple-element.26), channel_id=1, source_target_pairs={{0,16},{16,32},{32,48},{48,64},{64,80},{80,96},{96,112},{112,128},... | collective-permute-start | bytes 393224 | tf_op jit(solution)/shard_map/ppermute | solution.py:19
  32.7 4.5 %collective-permute-start.3 = (f32[128,8,2]{0,2,1:T(2,128)S(1)}, f32[128,8,2]{0,2,1:T(2,128)S(1)}, u32[]{:S(2)}, u32[]{:S(2)}) collective-permute-start(f32[128,8,2]{0,2,1:T(2,128)S(1)} %get-tuple-element.19), channel_id=1, source_target_pairs={{1,0},{2,1},{3,2},{4,3},{5,4},{6,5},{7,6},{8,7},{9,8},{10,9},{11,1... | collective-permute-start | bytes 24584 | tf_op jit(solution)/shard_map/ppermute | solution.py:20
  34.8 2.4 %collective-permute-start.2 = (f32[128,8,2]{0,2,1:T(2,128)S(1)}, f32[128,8,2]{0,2,1:T(2,128)S(1)}, u32[]{:S(2)}, u32[]{:S(2)}) collective-permute-start(f32[128,8,2]{0,2,1:T(2,128)S(1)} %get-tuple-element.18), channel_id=1, source_target_pairs={{0,1},{1,2},{2,3},{3,4},{4,5},{5,6},{6,7},{7,8},{8,9},{9,10},{10,1... | collective-permute-start | bytes 24584 | tf_op jit(solution)/shard_map/ppermute | solution.py:19
  37.3 3.2 %copy-start.7 = (f32[1,128]{1,0:T(1,128)S(1)}, f32[1,128]{1,0:T(1,128)}, u32[]{:S(2)}) copy-start(f32[1,128]{1,0:T(1,128)} %param.17) | copy-start | bytes 1540
  41.2 5.7 %collective-permute-start.5 = (f32[128,2,128]{0,2,1:T(8,128)S(1)}, f32[128,2,128]{0,2,1:T(8,128)S(1)}, u32[]{:S(2)}, u32[]{:S(2)}) collective-permute-start(f32[128,2,128]{0,2,1:T(8,128)S(1)} %get-tuple-element.25), channel_id=1, source_target_pairs={{16,0},{32,16},{48,32},{64,48},{80,64},{96,80},{112,96},{128,112},... | collective-permute-start | bytes 393224 | tf_op jit(solution)/shard_map/ppermute | solution.py:20
  43.2 9.6 %collective-permute-start.4 = (f32[128,2,128]{0,2,1:T(8,128)S(1)}, f32[128,2,128]{0,2,1:T(8,128)S(1)}, u32[]{:S(2)}, u32[]{:S(2)}) collective-permute-start(f32[128,2,128]{0,2,1:T(8,128)S(1)} %get-tuple-element.24), channel_id=1, source_target_pairs={{0,16},{16,32},{32,48},{48,64},{64,80},{80,96},{96,112},{112,128},... | collective-permute-start | bytes 393224 | tf_op jit(solution)/shard_map/ppermute | solution.py:19
  52.8 4.8 %collective-permute-start.7 = (f32[128,8,2]{0,2,1:T(2,128)S(1)}, f32[128,8,2]{0,2,1:T(2,128)S(1)}, u32[]{:S(2)}, u32[]{:S(2)}) collective-permute-start(f32[128,8,2]{0,2,1:T(2,128)S(1)} %get-tuple-element.17), channel_id=1, source_target_pairs={{1,0},{2,1},{3,2},{4,3},{5,4},{6,5},{7,6},{8,7},{9,8},{10,9},{11,1... | collective-permute-start | bytes 24584 | tf_op jit(solution)/shard_map/ppermute | solution.py:20
  56.7 1.2 collective-permute-start.6
  59.0 18.5 %copy-start.1 = (f32[4,128]{1,0:T(4,128)S(1)}, f32[4,128]{1,0:T(4,128)}, u32[]{:S(2)}) copy-start(f32[4,128]{1,0:T(4,128)} %param.18) | copy-start | bytes 6148
  61.7 5.7 %collective-permute-start.9 = (f32[128,2,128]{0,2,1:T(8,128)S(1)}, f32[128,2,128]{0,2,1:T(8,128)S(1)}, u32[]{:S(2)}, u32[]{:S(2)}) collective-permute-start(f32[128,2,128]{0,2,1:T(8,128)S(1)} %get-tuple-element.23), channel_id=1, source_target_pairs={{16,0},{32,16},{48,32},{64,48},{80,64},{96,80},{112,96},{128,112},... | collective-permute-start | bytes 393224 | tf_op jit(solution)/shard_map/ppermute | solution.py:20
  63.6 9.6 %collective-permute-start.8 = (f32[128,2,128]{0,2,1:T(8,128)S(1)}, f32[128,2,128]{0,2,1:T(8,128)S(1)}, u32[]{:S(2)}, u32[]{:S(2)}) collective-permute-start(f32[128,2,128]{0,2,1:T(8,128)S(1)} %get-tuple-element.22), channel_id=1, source_target_pairs={{0,16},{16,32},{32,48},{48,64},{64,80},{80,96},{96,112},{112,128},... | collective-permute-start | bytes 393224 | tf_op jit(solution)/shard_map/ppermute | solution.py:19
  73.2 5.1 %collective-permute-start.11 = (f32[128,8,2]{0,2,1:T(2,128)S(1)}, f32[128,8,2]{0,2,1:T(2,128)S(1)}, u32[]{:S(2)}, u32[]{:S(2)}) collective-permute-start(f32[128,8,2]{0,2,1:T(2,128)S(1)} %get-tuple-element.15), channel_id=1, source_target_pairs={{1,0},{2,1},{3,2},{4,3},{5,4},{6,5},{7,6},{8,7},{9,8},{10,9},{11,1... | collective-permute-start | bytes 24584 | tf_op jit(solution)/shard_map/ppermute | solution.py:20
  77.5 1.2 collective-permute-start.10
  82.5 5.7 %collective-permute-start.13 = (f32[128,2,128]{0,2,1:T(8,128)S(1)}, f32[128,2,128]{0,2,1:T(8,128)S(1)}, u32[]{:S(2)}, u32[]{:S(2)}) collective-permute-start(f32[128,2,128]{0,2,1:T(8,128)S(1)} %get-tuple-element.21), channel_id=1, source_target_pairs={{16,0},{32,16},{48,32},{64,48},{80,64},{96,80},{112,96},{128,112},... | collective-permute-start | bytes 393224 | tf_op jit(solution)/shard_map/ppermute | solution.py:20
  84.4 9.6 %collective-permute-start.12 = (f32[128,2,128]{0,2,1:T(8,128)S(1)}, f32[128,2,128]{0,2,1:T(8,128)S(1)}, u32[]{:S(2)}, u32[]{:S(2)}) collective-permute-start(f32[128,2,128]{0,2,1:T(8,128)S(1)} %get-tuple-element.20), channel_id=1, source_target_pairs={{0,16},{16,32},{32,48},{48,64},{64,80},{80,96},{96,112},{112,128},... | collective-permute-start | bytes 393224 | tf_op jit(solution)/shard_map/ppermute | solution.py:19
  94.1 5.4 %collective-permute-start.15 = (f32[128,8,2]{0,2,1:T(2,128)S(1)}, f32[128,8,2]{0,2,1:T(2,128)S(1)}, u32[]{:S(2)}, u32[]{:S(2)}) collective-permute-start(f32[128,8,2]{0,2,1:T(2,128)S(1)} %get-tuple-element.13), channel_id=1, source_target_pairs={{1,0},{2,1},{3,2},{4,3},{5,4},{6,5},{7,6},{8,7},{9,8},{10,9},{11,1... | collective-permute-start | bytes 24584 | tf_op jit(solution)/shard_map/ppermute | solution.py:20
  98.7 1.2 collective-permute-start.14
  99.9 20.7 %copy-start.6 = (s32[512]{0:T(512)S(1)}, s32[512]{0:T(512)}, u32[]{:S(2)}) copy-start(s32[512]{0:T(512)} %param.23) | copy-start | bytes 6148
  99.9 20.7 %copy-start.3 = (f32[3,512]{1,0:T(4,128)S(1)}, f32[3,512]{1,0:T(4,128)}, u32[]{:S(2)}) copy-start(f32[3,512]{1,0:T(4,128)} %param.22) | copy-start | bytes 18436
  102.0 39.8 %copy-start.4 = (f32[128,4]{0,1:T(4,128)S(1)}, f32[128,4]{0,1:T(4,128)}, u32[]{:S(2)}) copy-start(f32[128,4]{0,1:T(4,128)} %param.19) | copy-start | bytes 6148
  103.1 40.6 %copy-start.5 = (f32[3,128]{1,0:T(4,128)S(1)}, f32[3,128]{1,0:T(4,128)}, u32[]{:S(2)}) copy-start(f32[3,128]{1,0:T(4,128)} %param.20) | copy-start | bytes 4612
  103.7 41.9 %copy-start.2 = (s32[3,512]{1,0:T(4,128)S(1)}, s32[3,512]{1,0:T(4,128)}, u32[]{:S(2)}) copy-start(s32[3,512]{1,0:T(4,128)} %param.21) | copy-start | bytes 18436
  104.0 6.0 %collective-permute-start.16 = (f32[4,512]{1,0:T(4,128)S(1)}, f32[4,512]{1,0:T(4,128)S(1)}, u32[]{:S(2)}, u32[]{:S(2)}) collective-permute-start(f32[4,512]{1,0:T(4,128)S(1)} %fusion.17), channel_id=1, source_target_pairs={{0,512},{1,513},{2,514},{3,515},{4,516},{5,517},{6,518},{7,519},{8... | collective-permute-start | bytes 24584 | tf_op jit(solution)/shard_map/ppermute | solution.py:28
  110.7 18.8 %all-to-all-start = ((f32[16,4,512]{2,1,0:T(4,128)}), f32[16,4,512]{2,1,0:T(4,128)S(1)}, u32[]{:S(2)}, u32[]{:S(2)}) async-start(f32[16,4,512]{2,1,0:T(4,128)} %broadcast_in_dim.31), calls=%async_computation | async-start | bytes 262144 | tf_op jit(solution)/shard_map/all_to_all | solution.py:33
  144.0 8.3 %collective-permute-start.17 = (f32[3,512]{1,0:T(4,128)S(1)}, f32[3,512]{1,0:T(4,128)S(1)}, u32[]{:S(2)}, u32[]{:S(2)}) collective-permute-start(f32[3,512]{1,0:T(4,128)S(1)} %fusion.15), channel_id=1, source_target_pairs={{512,0},{513,1},{514,2},{515,3},{516,4},{517,5},{518,6},{519,7},{5... | collective-permute-start | bytes 18440 | tf_op jit(solution)/shard_map/ppermute | solution.py:28
  175.0 13.5 %all-to-all-start.1 = ((f32[16,3,512]{2,1,0:T(4,128)}), f32[16,3,512]{2,1,0:T(4,128)S(1)}, u32[]{:S(2)}, u32[]{:S(2)}) async-start(f32[16,3,512]{2,1,0:T(4,128)} %bitcast.51), calls=%async_computation.1 | async-start | bytes 262144 | tf_op jit(solution)/shard_map/all_to_all | solution.py:55
where the time goes:
time: 190 us; the launch traced here: 189 us
  starting transfers between devices  76 us (40%)
  waiting for transfers between devices  53.3 us (28%)
  local copies, waits for them, and re-layouts  33.1 us (17%)
  other arithmetic  20 us (11%)
  matrix products  5.47 us (3%)
    ppermute x8, starting transfers between devices, padded_2(): after = lax.ppermute(first, axis, down)  41.9 us
    ppermute x8, waiting for transfers between devices, padded_2(): before = lax.ppermute(last, axis, up)  24.5 us
    scatter-add x3, other arithmetic, local(): partial_sum.at[:, sources[k]].add(remap_weights[k][None, :] * surface)  18.7 us
    ppermute x8, starting transfers between devices, padded_2(): before = lax.ppermute(last, axis, up)  13.1 us
    gather x12, local copies, waits for them, and re-layouts, linked_sum(): total = total + jnp.take(flat, links[k], axis=1)  12.5 us
    all_to_all x1, starting transfers between devices, copy_for_each(): return lax.all_to_all(copies, axis, split_axis=0, concat_axis=0, tiled=True)  9.95 us
    gather x3, local copies, waits for them, and re-layouts, local(): jnp.take(slab, sources[k], axis=1)  9.65 us
    all_to_all x1, waiting for transfers between devices, copy_for_each(): return lax.all_to_all(copies, axis, split_axis=0, concat_axis=0, tiled=True)  8.83 us
  transfers between devices with their start and end apart: 20, of which 18 were waited for; matrix products, arithmetic and copies ran while one was open for 2% of the time, Pallas kernels for 0%

commit v1 on v0

v1 whole, which is shorter than its diff:
```python
import jax
import jax.numpy as jnp
from jax import lax
from jax.experimental import pallas as pl
from jax.experimental.pallas import tpu as pltpu
from jax.sharding import PartitionSpec as P

LA = 90
LEV = 128
CELLS = 512
BS = 128
STEPS = 4
RUN = 4
COLS = 32
ROWS = 16
SLOTS = 768
EXT = BS + 4
MESH = pl.DeviceIdType.MESH
F32 = jnp.float32
BF16 = jnp.bfloat16


def exact_dot(a, b, dims):
    return lax.dot_general(
        a, b, (dims, ((), ())), precision=lax.Precision.HIGHEST, preferred_element_type=F32
    )


def fast_dot(a, b, dims):
    return lax.dot_general(a, b, (dims, ((), ())), preferred_element_type=F32)


NN = ((1,), (0,))
NT = ((1,), (1,))


def pieces(x):
    high = x.astype(BF16)
    return high, (x - high.astype(F32)).astype(BF16)


def rows8(x):
    return jnp.concatenate([x, jnp.zeros((8 - x.shape[0], x.shape[1]), x.dtype)], axis=0)


def iota(shape, dim):
    return lax.broadcasted_iota(jnp.int32, shape, dim)


def lane_roll(x, shift):
    shift = shift % x.shape[1]
    return x if shift == 0 else pltpu.roll(x, shift, 1)


def regroup(parts, n):
    width = parts[0].shape[1] // n
    group = iota(parts[0].shape, 1) // width
    out = []
    for b in range(n):
        total = lane_roll(parts[0], -b * width)
        for a in range(1, n):
            total = jnp.where(group == a, lane_roll(parts[a], (a - b) * width), total)
        out.append(total)
    return out


def body(
    n_zone,
    n_sub,
    cs_in,
    nb_in,
    mix_in,
    rate_in,
    fm_in,
    force_in,
    rm_in,
    src_in,
    rw_in,
    wet_in,
    ns_out,
    cpl_out,
    start,
    nb,
    mixing,
    rate,
    fm,
    force,
    rm,
    src,
    rw,
    wet,
    vt,
    idq,
    nidx,
    cnt,
    vx,
    edge,
    vsum,
    w2,
    oh,
    fx,
    fin,
    ft,
    ftab,
    rt,
    bmsg,
    bin_,
    pbuf,
    cin,
    nsb,
    cplb,
    in_sem,
    t_send,
    t_recv,
    h_send,
    h_recv,
    f_send,
    f_recv,
    r_send,
    r_recv,
    x_send,
    x_recv,
    b_send,
    b_recv,
    o_sem,
):
    grp = lax.axis_index("grp")
    reg = lax.axis_index("reg")
    s = lax.axis_index("sub")
    z = reg // RUN
    j = reg % RUN
    odd = s % 2
    ocean = grp == 1
    atmos = grp == 0

    def chunk_of(place):
        return jnp.where(odd == 1, RUN - 1 - place, place)

    q = chunk_of(j)
    z_up = lax.rem(z + n_zone - 1, n_zone)
    z_down = lax.rem(z + 1, n_zone)
    s_before = lax.rem(s + n_sub - 1, n_sub)
    s_after = lax.rem(s + 1, n_sub)
    l_j = jnp.where(q == 0, j, chunk_of(q - 1))
    l_s = jnp.where(q == 0, s_before, s)
    r_j = jnp.where(q == RUN - 1, j, chunk_of(q + 1))
    r_s = jnp.where(q == RUN - 1, s_after, s)

    def at(g, zone, place, sub):
        return (g, zone * RUN + place, sub)

    run_peers = [lax.rem(j + d, RUN) for d in range(RUN)]
    sub_peers = [lax.rem(s + d, n_sub) for d in range(n_sub)]
    halo_peers = [
        at(grp, z_up, j, s),
        at(grp, z_down, j, s),
        at(grp, z, l_j, l_s),
        at(grp, z, r_j, r_s),
        at(grp, z_up, l_j, l_s),
        at(grp, z_up, r_j, r_s),
        at(grp, z_down, l_j, l_s),
        at(grp, z_down, r_j, r_s),
    ]

    barrier = pltpu.get_barrier_semaphore()
    greeted = [at(grp, z, p, s) for p in run_peers[1:]]
    greeted += [at(1 - grp, z, p, s) for p in run_peers]
    greeted += [at(grp, z, j, p) for p in sub_peers[1:]]
    greeted += halo_peers
    for device in greeted:
        pl.semaphore_signal(barrier, inc=1, device_id=device, device_id_type=MESH)

    loads = [
        pltpu.make_async_copy(a, b, in_sem.at[n])
        for n, (a, b) in enumerate(
            [
                (cs_in.at[0], start),
                (nb_in, nb),
                (mix_in.at[0], mixing),
                (rate_in, rate),
                (fm_in, fm),
                (force_in, force),
                (rm_in, rm),
                (src_in, src),
                (rw_in, rw),
                (wet_in, wet),
            ]
        )
    ]
    for load in loads:
        load.start()

    lane = iota((1, LEV), 1)
    keep = jnp.logical_or(lane < LA, ocean).astype(F32)

    loads[1].wait()
    lanes_rq = [
        rows8(jnp.concatenate([nb[k, :, pl.ds(r * BS, BS)] for k in range(3)], axis=0))
        for r in range(RUN)
    ]
    for c, block in enumerate(regroup(lanes_rq, RUN)):
        idq[c] = block

    loads[0].wait()
    for r in range(RUN):
        vt[r] = jnp.transpose(start[:, r * BS : (r + 1) * BS]) * keep

    pl.semaphore_wait(barrier, len(greeted))

    def remote(source, target, send, recv, device):
        return pltpu.make_async_remote_copy(
            src_ref=source,
            dst_ref=target,
            send_sem=send,
            recv_sem=recv,
            device_id=device,
            device_id_type=MESH,
        )

    index_copies, state_copies = [], []
    for d in range(1, RUN):
        peer = run_peers[d]
        c = chunk_of(peer)
        index_copies.append(
            remote(idq.at[c], nidx.at[j], t_send.at[0, d], t_recv.at[0, d], at(grp, z, peer, s))
        )
        state_copies.append(
            remote(
                vt.at[:, pl.ds(pl.multiple_of(c * COLS, COLS), COLS), :],
                vx.at[0, pl.ds(j * RUN, RUN)],
                t_send.at[1, d],
                t_recv.at[1, d],
                at(grp, z, peer, s),
            )
        )
    for copy in index_copies + state_copies:
        copy.start()
    nidx[j] = idq[q]
    for r in range(RUN):
        vx[0, j * RUN + r] = vt[r, pl.ds(pl.multiple_of(q * COLS, COLS), COLS), :]
    for n in range(STEPS):
        vx[n, 23] = jnp.zeros((COLS, LEV), F32)
    vsum[...] = jnp.zeros_like(vsum)

    loads[2].wait()
    m_high, m_low = pieces(jnp.transpose(mixing[...]))
    for a in range(2):
        w2[a * LEV : (a + 1) * LEV, 0:LEV] = m_high
        w2[a * LEV : (a + 1) * LEV, LEV : 2 * LEV] = m_low

    loads[7].wait()
    place = src[...]
    owner = (place // CELLS) * RUN + (place % BS) // COLS
    inside = ((place % CELLS) // BS) * COLS + place % COLS
    for k in range(3):
        hot = (iota((BS, CELLS), 0) == inside[k : k + 1, :]).astype(F32).astype(BF16)
        oh[0:BS, k * CELLS : (k + 1) * CELLS] = hot
        oh[BS : 2 * BS, k * CELLS : (k + 1) * CELLS] = hot

    for copy in index_copies:
        copy.wait_recv()
    for i in range(RUN):
        link = nidx[i]
        e_row = jnp.zeros_like(link)
        for a in range(1, 8):
            e_row = e_row + (link >= a * EXT).astype(jnp.int32)
        row = e_row + (i * RUN - 2)
        col = link - e_row * EXT - 2 - q * COLS
        above, below = row < 0, row >= ROWS
        left, right = col < 0, col >= COLS
        slot = row * COLS + col
        slot = jnp.where(above, (row + 2) * COLS + col + 512, slot)
        slot = jnp.where(below, (row - ROWS) * COLS + col + 576, slot)
        slot_l = row * 2 + col + 642
        slot_l = jnp.where(above, (row + 4) * 2 + col + 706, slot_l)
        slot_l = jnp.where(below, (row - ROWS) * 2 + col + 722, slot_l)
        slot_r = row * 2 + col - COLS + 672
        slot_r = jnp.where(above, (row + 4) * 2 + col - COLS + 712, slot_r)
        slot_r = jnp.where(below, (row - ROWS) * 2 + col - COLS + 728, slot_r)
        slot = jnp.where(left, slot_l, jnp.where(right, slot_r, slot)).astype(F32)
        tall = jnp.concatenate([slot, jnp.zeros((BS - 8, BS), F32)], axis=0)
        slot_t = jnp.transpose(tall)
        for b in range(SLOTS // BS):
            here = (iota((BS, BS), 1) + b * BS).astype(F32)
            total = (slot_t[:, 0:1] == here).astype(F32)
            for k in range(1, 3):
                total = total + (slot_t[:, k : k + 1] == here).astype(F32)
            cnt[i * BS : (i + 1) * BS, b * BS : (b + 1) * BS] = total.astype(BF16)

    loads[3].wait()
    for copy in state_copies:
        copy.wait_recv()

    def step(n, carry):
        for row in range(ROWS):
            spot = pl.ds(2 * (row % 4), 2)
            edge[n, 0, row // 4, spot, :] = vx[n, row, 0:2, :]
            edge[n, 1, row // 4, spot, :] = vx[n, row, COLS - 2 : COLS, :]
        routes = [
            (vx.at[n, pl.ds(0, 2)], vx.at[n, pl.ds(18, 2)]),
            (vx.at[n, pl.ds(14, 2)], vx.at[n, pl.ds(16, 2)]),
            (edge.at[n, 0], vx.at[n, 21]),
            (edge.at[n, 1], vx.at[n, 20]),
            (edge.at[n, 0, 0], vx.at[n, 22, pl.ds(24, 8)]),
            (edge.at[n, 1, 0], vx.at[n, 22, pl.ds(16, 8)]),
            (edge.at[n, 0, 3], vx.at[n, 22, pl.ds(8, 8)]),
            (edge.at[n, 1, 3], vx.at[n, 22, pl.ds(0, 8)]),
        ]
        copies = []
        for d, (source, target) in enumerate(routes):
            if d in (2, 3):
                for part in range(4):
                    copies.append(
                        remote(
                            source.at[part],
                            target.at[pl.ds(8 * part, 8)],
                            h_send.at[n, d * 4 + part],
                            h_recv.at[n, d * 4 + part],
                            halo_peers[d],
                        )
                    )
            else:
                copies.append(
                    remote(source, target, h_send.at[n, d], h_recv.at[n, d], halo_peers[d])
                )
        for copy in copies:
            copy.start()
        field = vx[n, 0:ROWS].reshape(CELLS, LEV)
        high, low = pieces(field)
        acc = fast_dot(cnt[:, 0:CELLS], jnp.concatenate([high, low], axis=1), NN)
        for copy in copies:
            copy.wait_recv()
        high, low = pieces(vx[n, ROWS:24].reshape(SLOTS - CELLS, LEV))
        acc = acc + fast_dot(cnt[:, CELLS:SLOTS], jnp.concatenate([high, low], axis=1), NN)
        total = acc[:, 0:LEV] + acc[:, LEV : 2 * LEV]
        spread = field + rate[...] * (total - 3.0 * field)
        high, low = pieces(spread)
        mixed = fast_dot(jnp.concatenate([high, low], axis=1), w2[...], NN)
        new = keep * (spread + mixed[:, 0:LEV] + mixed[:, LEV : 2 * LEV])
        vx[n + 1, 0:ROWS] = new.reshape(ROWS, COLS, LEV)
        vsum[...] = vsum[...] + new
        for copy in copies:
            copy.wait_send()
        return carry

    n_steps = jnp.where(ocean, 1, STEPS)
    lax.fori_loop(0, n_steps, step, 0)

    def flux_copies(g):
        return [
            remote(
                fx.at[i],
                fin.at[q],
                f_send.at[g, i],
                f_recv.at[j],
                at(g, z, i, s),
            )
            for i in range(RUN)
        ]

    loads[4].wait()

    @pl.when(atmos)
    def _():
        flux = exact_dot(rows8(fm[...]), vsum[...], NT) * (1.0 / STEPS)
        for i in range(RUN):
            fx[i] = flux[:, i * BS : (i + 1) * BS]
        for i, copy in enumerate(flux_copies(0)):

            @pl.when(j != i)
            def _(copy=copy):
                copy.start()

        for copy in flux_copies(1):
            copy.start()
        fin[q] = fx[j]

    last = n_steps
    back_copies = []
    for d in range(1, RUN):
        peer = run_peers[d]
        back_copies.append(
            remote(
                vx.at[last, pl.ds(peer * RUN, RUN)],
                rt.at[:, pl.ds(pl.multiple_of(q * COLS, COLS), COLS), :],
                r_send.at[d],
                r_recv.at[d],
                at(grp, z, peer, s),
            )
        )
    for copy in back_copies:
        copy.start()
    for r in range(RUN):
        rt[r, pl.ds(pl.multiple_of(q * COLS, COLS), COLS), :] = vx[last, j * RUN + r]

    loads[5].wait()
    loads[6].wait()
    loads[8].wait()
    loads[9].wait()
    to_atmos = remote(bmsg, bin_, b_send, b_recv, at(1 - grp, z, j, s))
    force_t = rows8(force[...])
    pushed_t = force_t + exact_dot(force_t, mixing[...], NT)

    @pl.when(ocean)
    def _():
        for copy in back_copies:
            copy.wait_recv()
        returns = rows8(rm[...])
        base = exact_dot(returns, rt[...].reshape(CELLS, LEV), NT)
        gains = jnp.zeros((8, BS), F32)
        for f in range(4):
            gain = jnp.sum(returns * pushed_t[f : f + 1, :], axis=1, keepdims=True)
            gains = jnp.where(iota((8, BS), 1) == f, gain, gains)
        bmsg[:, 0:CELLS] = base
        bmsg[:, CELLS : CELLS + BS] = gains
        bin_[:, 0:CELLS] = base
        bin_[:, CELLS : CELLS + BS] = gains
        to_atmos.start()

    for i in range(RUN):

        @pl.when(jnp.logical_or(ocean, j != i))
        def _(i=i):
            remote(fx.at[i], fin.at[i], f_send.at[0, i], f_recv.at[i], at(1 - grp, z, i, s)).wait_recv()

    for c in range(RUN):
        ft[c * 4 : (c + 1) * 4, :] = fin[c, 0:4, :]
    ftab[s] = ft[...]

    def over_sub(source_of, table, leg):
        return [
            remote(
                source_of(sub_peers[d]),
                table.at[s],
                x_send.at[leg, d],
                x_recv.at[leg, d],
                at(grp, z, j, sub_peers[d]),
            )
            for d in range(1, n_sub)
        ]

    gather_copies = over_sub(lambda peer: ft, ftab, 0)
    for copy in gather_copies:
        copy.start()
    for copy in gather_copies:
        copy.wait_recv()

    n_rows = n_sub * ROWS
    high, low = pieces(ftab[...].reshape(n_rows, BS))
    table = jnp.concatenate([high, low], axis=1)
    row_owner = iota((n_rows, CELLS), 0) // 4
    ocean_flux = jnp.zeros((8, CELLS), F32)
    for k in range(3):
        taken = fast_dot(table, oh[:, k * CELLS : (k + 1) * CELLS], NN)
        taken = jnp.where(row_owner == owner[k : k + 1, :], taken, 0.0)
        taken = taken.reshape(n_rows // 8, 8, CELLS).sum(axis=0)
        ocean_flux = ocean_flux + rw[k : k + 1, :] * taken
    ocean_flux = ocean_flux + pltpu.roll(ocean_flux, 4, 0)

    @pl.when(atmos)
    def _():
        to_atmos.wait_recv()

    wet_f = wet[...].astype(F32)
    surface = bin_[:, 0:CELLS]
    for f in range(4):
        gain = bin_[:, CELLS + f : CELLS + f + 1]
        surface = surface + gain * ocean_flux[f : f + 1, :]
    surface = surface * wet_f
    surface = surface + pltpu.roll(surface, 4, 0)
    sums = None
    for k in range(3):
        high, low = pieces(surface * rw[k : k + 1, :])
        mine = row_owner == owner[k : k + 1, :]
        spread_out = []
        for piece in (high, low):
            tall = jnp.broadcast_to(piece.astype(F32)[None], (n_rows // 8, 8, CELLS))
            spread_out.append(jnp.where(mine, tall.reshape(n_rows, CELLS), 0.0).astype(BF16))
        part = fast_dot(
            jnp.concatenate(spread_out, axis=0), oh[0:BS, k * CELLS : (k + 1) * CELLS], NT
        )
        part = part[0:n_rows] + part[n_rows : 2 * n_rows]
        sums = part if sums is None else sums + part
    pbuf[...] = sums.reshape(n_sub, ROWS, BS)
    sum_copies = over_sub(lambda peer: pbuf.at[peer], cin, 1)
    for copy in sum_copies:
        copy.start()
    cin[s] = pbuf[s]

    @pl.when(atmos)
    def _():
        for copy in back_copies:
            copy.wait_recv()
        for r in range(RUN):
            nsb[:, r * BS : (r + 1) * BS] = jnp.transpose(rt[r])

    @pl.when(ocean)
    def _():
        columns = jnp.transpose(jnp.concatenate([pushed_t, jnp.zeros((BS - 8, BS), F32)], axis=0))
        for r in range(RUN):
            part = slice(r * BS, (r + 1) * BS)
            forced = jnp.transpose(rt[r])
            for f in range(4):
                forced = forced + columns[:, f : f + 1] * ocean_flux[f : f + 1, part]
            old = start[:, part]
            nsb[:, part] = old + wet_f[:, part] * (forced - old)

    out_state = pltpu.make_async_copy(nsb, ns_out.at[0], o_sem.at[0])
    out_state.start()

    for copy in sum_copies:
        copy.wait_recv()
    summed = cin[...].sum(axis=0)
    by_chunk = [rows8(summed[c * 4 : (c + 1) * 4, :]) for c in range(RUN)]
    for r, block in enumerate(regroup(by_chunk, RUN)):
        cplb[:, r * BS : (r + 1) * BS] = block[0:3, :]
    out_coupled = pltpu.make_async_copy(cplb, cpl_out, o_sem.at[1])
    out_coupled.start()

    for copy in index_copies + state_copies + back_copies + gather_copies + sum_copies:
        copy.wait_send()

    @pl.when(atmos)
    def _():
        for i, copy in enumerate(flux_copies(0)):

            @pl.when(j != i)
            def _(copy=copy):
                copy.wait_send()

        for copy in flux_copies(1):
            copy.wait_send()

    @pl.when(ocean)
    def _():
        to_atmos.wait_send()

    out_state.wait()
    out_coupled.wait()


def local(
    column_state,
    neighbours,
    mixing,
    diffusivity,
    flux_map,
    force_map,
    return_map,
    sources,
    remap_weights,
    wet,
):
    n_zone = lax.axis_size("reg") // RUN
    n_sub = lax.axis_size("sub")
    vmem, dma = pltpu.VMEM, pltpu.SemaphoreType.DMA
    i32 = jnp.int32
    scratch = [
        vmem((LEV, CELLS), F32),
        vmem((3, 1, CELLS), i32),
        vmem((LEV, LEV), F32),
        vmem((1, LEV), F32),
        vmem((4, LEV), F32),
        vmem((4, LEV), F32),
        vmem((3, LEV), F32),
        vmem((3, CELLS), i32),
        vmem((3, CELLS), F32),
        vmem((1, CELLS), i32),
        vmem((RUN, BS, LEV), F32),
        vmem((RUN, 8, BS), i32),
        vmem((RUN, 8, BS), i32),
        vmem((CELLS, SLOTS), BF16),
        vmem((STEPS + 1, 24, COLS, LEV), F32),
        vmem((STEPS, 2, 4, 8, LEV), F32),
        vmem((CELLS, LEV), F32),
        vmem((2 * LEV, 2 * LEV), BF16),
        vmem((2 * BS, 3 * CELLS), BF16),
        vmem((RUN, 8, BS), F32),
        vmem((RUN, 8, BS), F32),
        vmem((ROWS, BS), F32),
        vmem((n_sub, ROWS, BS), F32),
        vmem((RUN, BS, LEV), F32),
        vmem((8, CELLS + BS), F32),
        vmem((8, CELLS + BS), F32),
        vmem((n_sub, ROWS, BS), F32),
        vmem((n_sub, ROWS, BS), F32),
        vmem((LEV, CELLS), F32),
        vmem((3, CELLS), F32),
        dma((10,)),
        dma((2, RUN)),
        dma((2, RUN)),
        dma((STEPS, 16)),
        dma((STEPS, 16)),
        dma((2, RUN)),
        dma((RUN,)),
        dma((RUN,)),
        dma((RUN,)),
        dma((2, n_sub)),
        dma((2, n_sub)),
        dma(()),
        dma(()),
        dma((2,)),
    ]

    def kernel(*refs):
        body(n_zone, n_sub, *refs)

    anywhere = pl.BlockSpec(memory_space=pl.ANY)
    return pl.pallas_call(
        kernel,
        name="window",
        out_shape=(
            jax.ShapeDtypeStruct((1, LEV, CELLS), F32),
            jax.ShapeDtypeStruct((3, CELLS), F32),
        ),
        in_specs=[anywhere] * 10,
        out_specs=(anywhere, anywhere),
        scratch_shapes=scratch,
        compiler_params=pltpu.CompilerParams(
            collective_id=0, has_side_effects=True, vmem_limit_bytes=40 << 20
        ),
    )(
        column_state,
        neighbours.transpose(1, 0, 2),
        mixing,
        diffusivity,
        flux_map,
        force_map.T,
        return_map,
        sources,
        remap_weights,
        wet.reshape(1, CELLS),
    )


def solution(mesh):
    in_specs = (
        P("grp", None, ("reg", "sub")),
        P("grp", None, ("reg", "sub")),
        P("grp", None, None),
        P("grp", None),
        P(),
        P(),
        P(),
        P(None, ("reg", "sub")),
        P(None, ("reg", "sub")),
        P(("reg", "sub")),
    )
    out_specs = (P("grp", None, ("reg", "sub")), P(None, ("reg", "sub")))
    return jax.shard_map(local, mesh=mesh, in_specs=in_specs, out_specs=out_specs, check_vma=False)
```

time: 190 us -> 74.7 us (0.39)
  starting transfers between devices: 76 us -> 0 us
  Pallas kernels: 0 us -> 66.4 us
  waiting for transfers between devices: 53.3 us -> 0 us
  local copies, waits for them, and re-layouts: 33.1 us -> 7.21 us
  other arithmetic: 20 us -> 0 us
  matrix products: 5.47 us -> 0 us
    pallas_call x0 -> x1, Pallas kernels: none -> 66.4 us  [local(): pl.pallas_call(kernel, name='window', out_shape=(jax.ShapeDtypeStruct((1,...]
    ppermute x18 -> x0, starting transfers between devices: 61.7 us -> none  [the longest x8 41.9 us: padded_2(): after = lax.ppermute(first, axis, down)]
    ppermute x18 -> x0, waiting for transfers between devices: 36.2 us -> none  [the longest x8 24.5 us: padded_2(): before = lax.ppermute(last, axis, up)]
    gather x15 -> x0, local copies, waits for them, and re-layouts: 22.1 us -> none  [the longest x12 12.5 us: linked_sum(): total = total + jnp.take(flat, links[k], axis=1)]
    scatter-add x3 -> x0, other arithmetic: 18.7 us -> none  [local(): partial_sum.at[:, sources[k]].add(remap_weights[k][None, :] * surface)]
    all_to_all x2 -> x0, waiting for transfers between devices: 17.1 us -> none  [the longest x1 8.83 us: copy_for_each(): return lax.all_to_all(copies, axis, split_axis=0, concat_axis=0, tiled=True)]
    all_to_all x2 -> x0, starting transfers between devices: 14.3 us -> none  [the longest x1 9.95 us: copy_for_each(): return lax.all_to_all(copies, axis, split_axis=0, concat_axis=0, tiled=True)]
    dot_general x11 -> x0, matrix products: 5.47 us -> none  [the longest x5 2.4 us: mix(): jnp.dot(matrix, field, precision=lax.Precision.HIGHEST, preferred_element...]
  transfers between devices with their start and end apart: 20 -> 0, of which waited for: 18 -> 0; matrix products, arithmetic and copies ran while one was open for 2% -> 0% of each run, Pallas kernels for 0% -> 0%
where the time goes in v1:
time: 74.7 us; the launch traced here: 74.3 us
  Pallas kernels  66.4 us (89%)
  local copies, waits for them, and re-layouts  7.21 us (10%)
    pallas_call x1, Pallas kernels, local(): pl.pallas_call(kernel, name='window', out_shape=(jax.ShapeDtypeStruct((1,...  66.4 us
    unnamed x22, local copies, waits for them, and re-layouts  7.21 us

profile of v1, /device:TPU:1, one launch (start us, length us, event | category | flops | bytes accessed | tf_op | source)
XLA Modules:
  0.0 74.3 jit_solution(520387380858167477)
XLA Ops:
  0.6 0.0 copy-start.6
  0.6 0.0 copy-start.5
  0.7 0.0 copy-start.9
  0.7 0.7 copy-done.6
  1.3 0.0 copy-done.5
  1.3 0.0 copy-done.9
  1.3 0.0 copy-start
  1.3 0.9 %copy-done = f32[1,128,512]{2,1,0:T(8,128)S(1)} copy-done((f32[1,128,512]{2,1,0:T(8,128)S(1)}, f32[1,128,512]{2,1,0:T(8,128)}, u32[]{:S(2)}) %copy-start) | copy-done | bytes 262168
  2.3 0.0 copy-start.1
  2.3 0.8 %copy-done.1 = f32[1,128,128]{2,1,0:T(8,128)S(1)} copy-done((f32[1,128,128]{2,1,0:T(8,128)S(1)}, f32[1,128,128]{2,1,0:T(8,128)}, u32[]{:S(2)}) %copy-start.1) | copy-done | bytes 65560
  3.1 0.0 copy-start.2
  3.1 0.7 copy-done.2
  3.8 0.0 copy-start.3
  3.8 0.7 copy-done.3
  4.5 0.0 copy-start.4
  4.5 0.7 copy-done.4
  5.2 0.0 copy-start.7
  5.2 0.7 copy-done.7
  5.9 0.0 copy-start.8
  5.9 0.7 copy-done.8
  6.6 66.4 %window.1 = (f32[1,128,512]{2,1,0:T(8,128)S(1)}, f32[3,512]{1,0:T(4,128)S(1)}) custom-call(f32[1,128,512]{2,1,0:T(8,128)S(1)} %copy-done, s32[3,1,512]{2,1,0:T(1,128)S(1)} %bitcast.3, f32[1,128,128]{2,1,0:T(8,128)S(1)} %copy-done.1, f32[1,128]{1,0:T(1,128)S(1)} %copy-done.9, f32[4,128]{1,0:T(4,128)S(1)} %copy-done.5, f32[4,128]{1,0:T(4,128)S(1)} %bitcast.4, ...), custom_call_target="tpu_custom_call" | custom-call | tf_op jit(solution)/shard_map/window/pallas_call | solution.py:609
  73.0 0.7 copy.14
  73.7 0.6 copy.15
Async XLA Ops:
  0.6 0.7 copy-start.6
  0.6 0.7 copy-start.5
  0.7 0.7 copy-start.9
  1.3 1.0 %copy-start = (f32[1,128,512]{2,1,0:T(8,128)S(1)}, f32[1,128,512]{2,1,0:T(8,128)}, u32[]{:S(2)}) copy-start(f32[1,128,512]{2,1,0:T(8,128)} %refs_0_.1) | copy-start | bytes 786436
  2.3 0.8 %copy-start.1 = (f32[1,128,128]{2,1,0:T(8,128)S(1)}, f32[1,128,128]{2,1,0:T(8,128)}, u32[]{:S(2)}) copy-start(f32[1,128,128]{2,1,0:T(8,128)} %refs_2_.1) | copy-start | bytes 196612
  3.1 0.7 copy-start.2
  3.8 0.7 copy-start.3
  4.5 0.7 copy-start.4
  5.2 0.7 copy-start.7
  5.9 0.7 copy-start.8

commit v2 on v1

--- a/solution.py
+++ b/solution.py
@@ -13,7 +13,12 @@
 RUN = 4
 COLS = 32
 ROWS = 16
-SLOTS = 768
+RIM = 8
+EROWS = ROWS + 2 * RIM
+ECOLS = COLS + 2 * RIM
+BLOCK = 4 * ECOLS
+BAND = 8 * ECOLS
+TAG = 96
 EXT = BS + 4
 MESH = pl.DeviceIdType.MESH
 F32 = jnp.float32
@@ -92,10 +97,10 @@
     vt,
     idq,
     nidx,
+    lk,
     cnt,
     vx,
-    edge,
-    vsum,
+    sp,
     w2,
     oh,
     fx,
@@ -107,8 +112,6 @@
     bin_,
     pbuf,
     cin,
-    nsb,
-    cplb,
     in_sem,
     t_send,
     t_recv,
@@ -122,7 +125,6 @@
     x_recv,
     b_send,
     b_recv,
-    o_sem,
 ):
     grp = lax.axis_index("grp")
     reg = lax.axis_index("reg")
@@ -149,7 +151,7 @@
     def at(g, zone, place, sub):
         return (g, zone * RUN + place, sub)
 
-    run_peers = [lax.rem(j + d, RUN) for d in range(RUN)]
+    run_peers = [j, j + 1 - 2 * (j % 2), lax.rem(j + 2, RUN), RUN - 1 - j]
     sub_peers = [lax.rem(s + d, n_sub) for d in range(n_sub)]
     halo_peers = [
         at(grp, z_up, j, s),
@@ -192,18 +194,28 @@
 
     lane = iota((1, LEV), 1)
     keep = jnp.logical_or(lane < LA, ocean).astype(F32)
+    tagged = jnp.logical_and(lane >= TAG, lane < TAG + 3)
+    carried = jnp.logical_or(jnp.logical_or(lane < LA, ocean), tagged).astype(F32)
 
     loads[1].wait()
-    lanes_rq = [
-        rows8(jnp.concatenate([nb[k, :, pl.ds(r * BS, BS)] for k in range(3)], axis=0))
-        for r in range(RUN)
-    ]
-    for c, block in enumerate(regroup(lanes_rq, RUN)):
+    link = rows8(jnp.concatenate([nb[k] for k in range(3)], axis=0))
+    e_row = jnp.zeros_like(link)
+    for a in range(1, 8):
+        e_row = e_row + (link >= a * EXT).astype(jnp.int32)
+    cell = iota((8, CELLS), 1)
+    offset = ECOLS * (e_row - 2 - cell // BS) + (link - e_row * EXT - 2 - cell % BS)
+    offset = offset.astype(F32)
+    blocks = regroup([offset[:, r * BS : (r + 1) * BS] for r in range(RUN)], RUN)
+    for c, block in enumerate(blocks):
         idq[c] = block
 
     loads[0].wait()
+    tags = jnp.concatenate([offset, jnp.zeros((LEV - TAG - 8, CELLS), F32)], axis=0)
     for r in range(RUN):
-        vt[r] = jnp.transpose(start[:, r * BS : (r + 1) * BS]) * keep
+        part = slice(r * BS, (r + 1) * BS)
+        tall = jnp.where(ocean, start[TAG:LEV, part], tags[:, part])
+        tall = jnp.concatenate([start[0:TAG, part], tall], axis=0)
+        vt[r] = jnp.transpose(tall) * carried
 
     pl.semaphore_wait(barrier, len(greeted))
 
@@ -227,23 +239,51 @@
         state_copies.append(
             remote(
                 vt.at[:, pl.ds(pl.multiple_of(c * COLS, COLS), COLS), :],
-                vx.at[0, pl.ds(j * RUN, RUN)],
+                vx.at[0, pl.ds(RIM + j * RUN, RUN), pl.ds(RIM, COLS)],
                 t_send.at[1, d],
                 t_recv.at[1, d],
                 at(grp, z, peer, s),
             )
         )
-    for copy in index_copies + state_copies:
+
+    @pl.when(ocean)
+    def _():
+        for copy in index_copies:
+            copy.start()
+
+    for copy in state_copies:
         copy.start()
     nidx[j] = idq[q]
     for r in range(RUN):
-        vx[0, j * RUN + r] = vt[r, pl.ds(pl.multiple_of(q * COLS, COLS), COLS), :]
-    for n in range(STEPS):
-        vx[n, 23] = jnp.zeros((COLS, LEV), F32)
-    vsum[...] = jnp.zeros_like(vsum)
+        piece = vt[r, pl.ds(pl.multiple_of(q * COLS, COLS), COLS), :]
+        vx[0, RIM + j * RUN + r, RIM : RIM + COLS, :] = piece
+
+    def halo_copies(i):
+        rows = pl.ds(RIM + RUN * i, RUN)
+        up = i < 2
+        zone = jnp.where(up, z_up, z_down)
+        landing = pl.ds(jnp.where(up, EROWS - RIM + RUN * i, RUN * i - RIM), RUN)
+        inner, first, end = pl.ds(RIM, COLS), pl.ds(RIM, RIM), pl.ds(COLS, RIM)
+        before, after = pl.ds(0, RIM), pl.ds(RIM + COLS, RIM)
+        here = vx.at[0]
+        routes = [
+            (here.at[rows, inner], here.at[landing, inner], at(grp, zone, j, s)),
+            (here.at[rows, first], here.at[landing, after], at(grp, zone, l_j, l_s)),
+            (here.at[rows, end], here.at[landing, before], at(grp, zone, r_j, r_s)),
+            (here.at[rows, first], here.at[rows, after], at(grp, z, l_j, l_s)),
+            (here.at[rows, end], here.at[rows, before], at(grp, z, r_j, r_s)),
+        ]
+        return [
+            remote(source, target, h_send.at[kind, i], h_recv.at[kind, i], device)
+            for kind, (source, target, device) in enumerate(routes)
+        ]
+
+    for copy in halo_copies(j):
+        copy.start()
 
     loads[2].wait()
-    m_high, m_low = pieces(jnp.transpose(mixing[...]))
+    used = jnp.logical_or(iota((LEV, LEV), 0) < LA, ocean)
+    m_high, m_low = pieces(jnp.where(used, jnp.transpose(mixing[...]), 0.0))
     for a in range(2):
         w2[a * LEV : (a + 1) * LEV, 0:LEV] = m_high
         w2[a * LEV : (a + 1) * LEV, LEV : 2 * LEV] = m_low
@@ -257,94 +297,88 @@
         oh[0:BS, k * CELLS : (k + 1) * CELLS] = hot
         oh[BS : 2 * BS, k * CELLS : (k + 1) * CELLS] = hot
 
-    for copy in index_copies:
-        copy.wait_recv()
+    for slot, first in ((1, 0), (1, EROWS - 2), (3, 4), (3, EROWS - 6)):
+        spot = slice(first * ECOLS, (first + 2) * ECOLS)
+        sp[slot, spot, :] = jnp.zeros((2 * ECOLS, 2 * LEV), BF16)
+
+    loads[3].wait()
+    for d in range(1, RUN):
+        state_copies[d - 1].wait_recv()
+        for copy in halo_copies(run_peers[d]):
+            copy.start()
+
+    gap = iota((BLOCK, BAND), 1) - iota((BLOCK, BAND), 0) - 2 * ECOLS
+    gap = gap.astype(F32)
+
+    def count(b, offsets, first):
+        total = (offsets[:, first : first + 1] == gap).astype(F32)
+        for k in range(1, 3):
+            total = total + (offsets[:, first + k : first + k + 1] == gap).astype(F32)
+        cnt[b] = total.astype(BF16)
+
+    @pl.when(ocean)
+    def _():
+        for copy in index_copies:
+            copy.wait_recv()
+        lk[...] = jnp.zeros_like(lk)
+        for i in range(RUN):
+            tall = jnp.concatenate([nidx[i], jnp.zeros((BS - 8, BS), F32)], axis=0)
+            tall = jnp.transpose(tall)
+            for r in range(RUN):
+                lk[RIM + RUN * i + r, RIM : RIM + COLS, :] = tall[r * COLS : (r + 1) * COLS]
+
+        def one(b, carry):
+            count(b, lk[pl.ds(4 * b + 2, 4)].reshape(BLOCK, LEV), 0)
+            return carry
+
+        lax.fori_loop(0, 7, one, 0)
+
     for i in range(RUN):
-        link = nidx[i]
-        e_row = jnp.zeros_like(link)
-        for a in range(1, 8):
-            e_row = e_row + (link >= a * EXT).astype(jnp.int32)
-        row = e_row + (i * RUN - 2)
-        col = link - e_row * EXT - 2 - q * COLS
-        above, below = row < 0, row >= ROWS
-        left, right = col < 0, col >= COLS
-        slot = row * COLS + col
-        slot = jnp.where(above, (row + 2) * COLS + col + 512, slot)
-        slot = jnp.where(below, (row - ROWS) * COLS + col + 576, slot)
-        slot_l = row * 2 + col + 642
-        slot_l = jnp.where(above, (row + 4) * 2 + col + 706, slot_l)
-        slot_l = jnp.where(below, (row - ROWS) * 2 + col + 722, slot_l)
-        slot_r = row * 2 + col - COLS + 672
-        slot_r = jnp.where(above, (row + 4) * 2 + col - COLS + 712, slot_r)
-        slot_r = jnp.where(below, (row - ROWS) * 2 + col - COLS + 728, slot_r)
-        slot = jnp.where(left, slot_l, jnp.where(right, slot_r, slot)).astype(F32)
-        tall = jnp.concatenate([slot, jnp.zeros((BS - 8, BS), F32)], axis=0)
-        slot_t = jnp.transpose(tall)
-        for b in range(SLOTS // BS):
-            here = (iota((BS, BS), 1) + b * BS).astype(F32)
-            total = (slot_t[:, 0:1] == here).astype(F32)
-            for k in range(1, 3):
-                total = total + (slot_t[:, k : k + 1] == here).astype(F32)
-            cnt[i * BS : (i + 1) * BS, b * BS : (b + 1) * BS] = total.astype(BF16)
-
-    loads[3].wait()
-    for copy in state_copies:
-        copy.wait_recv()
-
-    def step(n, carry):
-        for row in range(ROWS):
-            spot = pl.ds(2 * (row % 4), 2)
-            edge[n, 0, row // 4, spot, :] = vx[n, row, 0:2, :]
-            edge[n, 1, row // 4, spot, :] = vx[n, row, COLS - 2 : COLS, :]
-        routes = [
-            (vx.at[n, pl.ds(0, 2)], vx.at[n, pl.ds(18, 2)]),
-            (vx.at[n, pl.ds(14, 2)], vx.at[n, pl.ds(16, 2)]),
-            (edge.at[n, 0], vx.at[n, 21]),
-            (edge.at[n, 1], vx.at[n, 20]),
-            (edge.at[n, 0, 0], vx.at[n, 22, pl.ds(24, 8)]),
-            (edge.at[n, 1, 0], vx.at[n, 22, pl.ds(16, 8)]),
-            (edge.at[n, 0, 3], vx.at[n, 22, pl.ds(8, 8)]),
-            (edge.at[n, 1, 3], vx.at[n, 22, pl.ds(0, 8)]),
-        ]
-        copies = []
-        for d, (source, target) in enumerate(routes):
-            if d in (2, 3):
-                for part in range(4):
-                    copies.append(
-                        remote(
-                            source.at[part],
-                            target.at[pl.ds(8 * part, 8)],
-                            h_send.at[n, d * 4 + part],
-                            h_recv.at[n, d * 4 + part],
-                            halo_peers[d],
-                        )
-                    )
-            else:
-                copies.append(
-                    remote(source, target, h_send.at[n, d], h_recv.at[n, d], halo_peers[d])
-                )
-        for copy in copies:
-            copy.start()
-        field = vx[n, 0:ROWS].reshape(CELLS, LEV)
-        high, low = pieces(field)
-        acc = fast_dot(cnt[:, 0:CELLS], jnp.concatenate([high, low], axis=1), NN)
-        for copy in copies:
+        for copy in halo_copies(i):
             copy.wait_recv()
-        high, low = pieces(vx[n, ROWS:24].reshape(SLOTS - CELLS, LEV))
-        acc = acc + fast_dot(cnt[:, CELLS:SLOTS], jnp.concatenate([high, low], axis=1), NN)
-        total = acc[:, 0:LEV] + acc[:, LEV : 2 * LEV]
-        spread = field + rate[...] * (total - 3.0 * field)
-        high, low = pieces(spread)
-        mixed = fast_dot(jnp.concatenate([high, low], axis=1), w2[...], NN)
-        new = keep * (spread + mixed[:, 0:LEV] + mixed[:, LEV : 2 * LEV])
-        vx[n + 1, 0:ROWS] = new.reshape(ROWS, COLS, LEV)
-        vsum[...] = vsum[...] + new
-        for copy in copies:
-            copy.wait_send()
+
+    @pl.when(atmos)
+    def _():
+        def one(b, carry):
+            count(b, vx[0, pl.ds(4 * b + 2, 4)].reshape(BLOCK, LEV), TAG)
+            return carry
+
+        lax.fori_loop(0, 7, one, 0)
+
+    for row in range(0, EROWS, 4):
+        high, low = pieces(vx[0, row : row + 4].reshape(BLOCK, LEV))
+        sp[0, row * ECOLS : (row + 4) * ECOLS, 0:LEV] = high
+        sp[0, row * ECOLS : (row + 4) * ECOLS, LEV : 2 * LEV] = low
+
+    def step(n, blocks):
+        for b in blocks:
+            row = 4 * b + 2
+            acc = fast_dot(cnt[b], sp[n, 4 * b * ECOLS : 4 * b * ECOLS + BAND, :], NN)
+            field = vx[n, row : row + 4].reshape(BLOCK, LEV)
+            total = acc[:, 0:LEV] + acc[:, LEV : 2 * LEV]
+            spread = field + rate[...] * (total - 3.0 * field)
+            high, low = pieces(spread)
+            mixed = fast_dot(jnp.concatenate([high, low], axis=1), w2[...], NN)
+            new = keep * (spread + mixed[:, 0:LEV] + mixed[:, LEV : 2 * LEV])
+            vx[n + 1, row : row + 4] = new.reshape(4, ECOLS, LEV)
+            high, low = pieces(new)
+            sp[n + 1, row * ECOLS : row * ECOLS + BLOCK, 0:LEV] = high
+            sp[n + 1, row * ECOLS : row * ECOLS + BLOCK, LEV : 2 * LEV] = low
+
+    def wide(n, carry):
+        step(n, range(7))
         return carry
 
+    def narrow(n, carry):
+        step(n, range(1, 6))
+        return carry
+
     n_steps = jnp.where(ocean, 1, STEPS)
-    lax.fori_loop(0, n_steps, step, 0)
+    lax.fori_loop(0, jnp.where(ocean, 1, 2), wide, 0)
+    lax.fori_loop(jnp.where(ocean, STEPS, 2), STEPS, narrow, 0)
+
+    def own(n):
+        return vx[n, RIM : RIM + ROWS, RIM : RIM + COLS, :].reshape(CELLS, LEV)
 
     def flux_copies(g):
         return [
@@ -362,7 +396,7 @@
 
     @pl.when(atmos)
     def _():
-        flux = exact_dot(rows8(fm[...]), vsum[...], NT) * (1.0 / STEPS)
+        flux = exact_dot(rows8(fm[...]), own(1) + own(2) + own(3) + own(4), NT) * (1.0 / STEPS)
         for i in range(RUN):
             fx[i] = flux[:, i * BS : (i + 1) * BS]
         for i, copy in enumerate(flux_copies(0)):
@@ -381,17 +415,22 @@
         peer = run_peers[d]
         back_copies.append(
             remote(
-                vx.at[last, pl.ds(peer * RUN, RUN)],
+                vx.at[last, pl.ds(RIM + peer * RUN, RUN), pl.ds(RIM, COLS)],
                 rt.at[:, pl.ds(pl.multiple_of(q * COLS, COLS), COLS), :],
                 r_send.at[d],
                 r_recv.at[d],
                 at(grp, z, peer, s),
             )
         )
-    for copy in back_copies:
-        copy.start()
+
+    @pl.when(ocean)
+    def _():
+        for copy in back_copies:
+            copy.start()
+
     for r in range(RUN):
-        rt[r, pl.ds(pl.multiple_of(q * COLS, COLS), COLS), :] = vx[last, j * RUN + r]
+        piece = vx[last, RIM + j * RUN + r, RIM : RIM + COLS, :]
+        rt[r, pl.ds(pl.multiple_of(q * COLS, COLS), COLS), :] = piece
 
     loads[5].wait()
     loads[6].wait()
@@ -442,6 +481,12 @@
     gather_copies = over_sub(lambda peer: ft, ftab, 0)
     for copy in gather_copies:
         copy.start()
+
+    @pl.when(atmos)
+    def _():
+        for copy in back_copies:
+            copy.start()
+
     for copy in gather_copies:
         copy.wait_recv()
 
@@ -492,7 +537,7 @@
         for copy in back_copies:
             copy.wait_recv()
         for r in range(RUN):
-            nsb[:, r * BS : (r + 1) * BS] = jnp.transpose(rt[r])
+            ns_out[0, :, r * BS : (r + 1) * BS] = jnp.transpose(rt[r])
 
     @pl.when(ocean)
     def _():
@@ -503,22 +548,20 @@
             for f in range(4):
                 forced = forced + columns[:, f : f + 1] * ocean_flux[f : f + 1, part]
             old = start[:, part]
-            nsb[:, part] = old + wet_f[:, part] * (forced - old)
-
-    out_state = pltpu.make_async_copy(nsb, ns_out.at[0], o_sem.at[0])
-    out_state.start()
+            ns_out[0, :, part] = old + wet_f[:, part] * (forced - old)
 
     for copy in sum_copies:
         copy.wait_recv()
     summed = cin[...].sum(axis=0)
     by_chunk = [rows8(summed[c * 4 : (c + 1) * 4, :]) for c in range(RUN)]
     for r, block in enumerate(regroup(by_chunk, RUN)):
-        cplb[:, r * BS : (r + 1) * BS] = block[0:3, :]
-    out_coupled = pltpu.make_async_copy(cplb, cpl_out, o_sem.at[1])
-    out_coupled.start()
-
-    for copy in index_copies + state_copies + back_copies + gather_copies + sum_copies:
+        cpl_out[:, r * BS : (r + 1) * BS] = block[0:3, :]
+
+    for copy in state_copies + back_copies + gather_copies + sum_copies:
         copy.wait_send()
+    for i in range(RUN):
+        for copy in halo_copies(i):
+            copy.wait_send()
 
     @pl.when(atmos)
     def _():
@@ -534,9 +577,8 @@
     @pl.when(ocean)
     def _():
         to_atmos.wait_send()
-
-    out_state.wait()
-    out_coupled.wait()
+        for copy in index_copies:
+            copy.wait_send()
 
 
 def local(
@@ -567,12 +609,12 @@
         vmem((3, CELLS), F32),
         vmem((1, CELLS), i32),
         vmem((RUN, BS, LEV), F32),
-        vmem((RUN, 8, BS), i32),
-        vmem((RUN, 8, BS), i32),
-        vmem((CELLS, SLOTS), BF16),
-        vmem((STEPS + 1, 24, COLS, LEV), F32),
-        vmem((STEPS, 2, 4, 8, LEV), F32),
-        vmem((CELLS, LEV), F32),
+        vmem((RUN, 8, BS), F32),
+        vmem((RUN, 8, BS), F32),
+        vmem((EROWS, ECOLS, LEV), F32),
+        vmem((7, BLOCK, BAND), BF16),
+        vmem((STEPS + 1, EROWS, ECOLS, LEV), F32),
+        vmem((STEPS + 1, EROWS * ECOLS, 2 * LEV), BF16),
         vmem((2 * LEV, 2 * LEV), BF16),
         vmem((2 * BS, 3 * CELLS), BF16),
         vmem((RUN, 8, BS), F32),
@@ -584,13 +626,11 @@
         vmem((8, CELLS + BS), F32),
         vmem((n_sub, ROWS, BS), F32),
         vmem((n_sub, ROWS, BS), F32),
-        vmem((LEV, CELLS), F32),
-        vmem((3, CELLS), F32),
         dma((10,)),
         dma((2, RUN)),
         dma((2, RUN)),
-        dma((STEPS, 16)),
-        dma((STEPS, 16)),
+        dma((5, RUN)),
+        dma((5, RUN)),
         dma((2, RUN)),
         dma((RUN,)),
         dma((RUN,)),
@@ -599,13 +639,11 @@
         dma((2, n_sub)),
         dma(()),
         dma(()),
-        dma((2,)),
     ]
 
     def kernel(*refs):
         body(n_zone, n_sub, *refs)
 
-    anywhere = pl.BlockSpec(memory_space=pl.ANY)
     return pl.pallas_call(
         kernel,
         name="window",
@@ -613,13 +651,13 @@
             jax.ShapeDtypeStruct((1, LEV, CELLS), F32),
             jax.ShapeDtypeStruct((3, CELLS), F32),
         ),
-        in_specs=[anywhere] * 10,
-        out_specs=(anywhere, anywhere),
+        in_specs=[pl.BlockSpec(memory_space=pltpu.HBM)] * 10,
+        out_specs=(pl.BlockSpec(memory_space=pltpu.VMEM),) * 2,
         scratch_shapes=scratch,
         compiler_params=pltpu.CompilerParams(
             collective_id=0, has_side_effects=True, vmem_limit_bytes=40 << 20
         ),
-    )(
+    )(*[pltpu.with_memory_space_constraint(a, pltpu.HBM) for a in (
         column_state,
         neighbours.transpose(1, 0, 2),
         mixing,
@@ -630,7 +668,7 @@
         sources,
         remap_weights,
         wet.reshape(1, CELLS),
-    )
+    )])
 
 
 def solution(mesh):

time: 74.7 us -> 61 us (0.82)
  Pallas kernels: 66.4 us -> 58.9 us
  local copies, waits for them, and re-layouts: 7.21 us -> 1.3 us
    pallas_call x1, Pallas kernels: 66.4 us -> 58.9 us  [local(): pl.pallas_call(kernel, name='window', out_shape=(jax.ShapeDtypeStruct((1,...]
    unnamed x22 -> x2, local copies, waits for them, and re-layouts: 7.21 us -> 1.3 us
where the time goes in v2:
time: 61 us; the launch traced here: 60.8 us
  Pallas kernels  58.9 us (97%)
  local copies, waits for them, and re-layouts  1.3 us (2%)
  between operations  0.64 us (1%)
    pallas_call x1, Pallas kernels, local(): pl.pallas_call(kernel, name='window', out_shape=(jax.ShapeDtypeStruct((1,...  58.9 us
    unnamed x2, local copies, waits for them, and re-layouts  1.3 us

profile of v2, /device:TPU:1, one launch (start us, length us, event | category | flops | bytes accessed | tf_op | source)
XLA Modules:
  0.0 60.8 jit_solution(2287604319610897318)
XLA Ops:
  0.6 58.9 %window.1 = (f32[1,128,512]{2,1,0:T(8,128)S(1)}, f32[3,512]{1,0:T(4,128)S(1)}) custom-call(f32[1,128,512]{2,1,0:T(8,128)} %refs_0_.1, s32[3,1,512]{2,1,0:T(1,128)} %bitcast.3, f32[1,128,128]{2,1,0:T(8,128)} %refs_2_.1, f32[1,128]{1,0:T(1,128)} %refs_3_.1, f32[4,128]{1,0:T(4,128)} %refs_4_.1, f32[4,128]{1,0:T(4,128)} %bitcast.4, f32[3,128]{1,0:T(4,128)} %refs_6_.1, ...), custom_call_target="tpu_custom_call" | custom-call | tf_op jit(solution)/shard_map/window/pallas_call | solution.py:647
  59.5 0.7 %copy.14 = f32[1,128,512]{2,1,0:T(8,128)} copy(f32[1,128,512]{2,1,0:T(8,128)S(1)} %get-tuple-element.4) | data formatting | bytes 524288
  60.2 0.6 copy.15

commit v3 on v2

--- a/solution.py
+++ b/solution.py
@@ -18,7 +18,9 @@
 ECOLS = COLS + 2 * RIM
 BLOCK = 4 * ECOLS
 BAND = 8 * ECOLS
-TAG = 96
+TAG = LA
+PACK = 96
+THIRD = PACK // 3
 EXT = BS + 4
 MESH = pl.DeviceIdType.MESH
 F32 = jnp.float32
@@ -176,7 +178,6 @@
         pltpu.make_async_copy(a, b, in_sem.at[n])
         for n, (a, b) in enumerate(
             [
-                (cs_in.at[0], start),
                 (nb_in, nb),
                 (mix_in.at[0], mixing),
                 (rate_in, rate),
@@ -189,15 +190,21 @@
             ]
         )
     ]
-    for load in loads:
+    columns = [
+        pltpu.make_async_copy(
+            cs_in.at[0, :, pl.ds(r * BS, BS)], start.at[:, pl.ds(r * BS, BS)], in_sem.at[9 + r]
+        )
+        for r in range(RUN)
+    ]
+    loads[0].start()
+    for r in (3, 0, 1, 2):
+        columns[r].start()
+    for load in loads[1:]:
         load.start()
 
     lane = iota((1, LEV), 1)
     keep = jnp.logical_or(lane < LA, ocean).astype(F32)
-    tagged = jnp.logical_and(lane >= TAG, lane < TAG + 3)
-    carried = jnp.logical_or(jnp.logical_or(lane < LA, ocean), tagged).astype(F32)
-
-    loads[1].wait()
+    loads[0].wait()
     link = rows8(jnp.concatenate([nb[k] for k in range(3)], axis=0))
     e_row = jnp.zeros_like(link)
     for a in range(1, 8):
@@ -205,17 +212,34 @@
     cell = iota((8, CELLS), 1)
     offset = ECOLS * (e_row - 2 - cell // BS) + (link - e_row * EXT - 2 - cell % BS)
     offset = offset.astype(F32)
-    blocks = regroup([offset[:, r * BS : (r + 1) * BS] for r in range(RUN)], RUN)
-    for c, block in enumerate(blocks):
-        idq[c] = block
-
-    loads[0].wait()
-    tags = jnp.concatenate([offset, jnp.zeros((LEV - TAG - 8, CELLS), F32)], axis=0)
-    for r in range(RUN):
-        part = slice(r * BS, (r + 1) * BS)
-        tall = jnp.where(ocean, start[TAG:LEV, part], tags[:, part])
-        tall = jnp.concatenate([start[0:TAG, part], tall], axis=0)
-        vt[r] = jnp.transpose(tall) * carried
+
+    @pl.when(ocean)
+    def _():
+        blocks = regroup([offset[:, r * BS : (r + 1) * BS] for r in range(RUN)], RUN)
+        for c, block in enumerate(blocks):
+            idq[c] = block
+        for r in range(RUN):
+            columns[r].wait()
+            vt[r] = jnp.transpose(start[:, r * BS : (r + 1) * BS])
+
+    @pl.when(atmos)
+    def _():
+        at_tag = TAG % 8
+        row = iota((8, BS), 0)
+        tags = pltpu.roll(offset, at_tag, 0)
+        packed = None
+        for r in (3, 0, 1, 2):
+            columns[r].wait()
+            part = slice(r * BS, (r + 1) * BS)
+            mixed_rows = jnp.where(row < at_tag + 3, tags[:, part], 0.0)
+            mixed_rows = jnp.where(row < at_tag, start[TAG - at_tag : PACK, part], mixed_rows)
+            tall = [start[0 : TAG - at_tag, part], mixed_rows, jnp.zeros((LEV - PACK, BS), F32)]
+            tall = jnp.transpose(jnp.concatenate(tall, axis=0))
+            if packed is None:
+                packed = tall
+            else:
+                tall = jnp.where(lane < PACK, tall, lane_roll(packed, PACK - r * THIRD))
+            vt[r] = tall
 
     pl.semaphore_wait(barrier, len(greeted))
 
@@ -229,40 +253,46 @@
             device_id_type=MESH,
         )
 
-    index_copies, state_copies = [], []
+    index_copies, state_copies, rest_copies = [], [], []
     for d in range(1, RUN):
         peer = run_peers[d]
         c = chunk_of(peer)
+        there = at(grp, z, peer, s)
         index_copies.append(
-            remote(idq.at[c], nidx.at[j], t_send.at[0, d], t_recv.at[0, d], at(grp, z, peer, s))
+            remote(idq.at[c], nidx.at[j], t_send.at[0, d], t_recv.at[0, d], there)
         )
-        state_copies.append(
-            remote(
-                vt.at[:, pl.ds(pl.multiple_of(c * COLS, COLS), COLS), :],
-                vx.at[0, pl.ds(RIM + j * RUN, RUN), pl.ds(RIM, COLS)],
-                t_send.at[1, d],
-                t_recv.at[1, d],
-                at(grp, z, peer, s),
+        cells = pl.ds(pl.multiple_of(c * COLS, COLS), COLS)
+        for part, copies, first, count in ((1, state_copies, 0, 3), (2, rest_copies, 3, 1)):
+            copies.append(
+                remote(
+                    vt.at[pl.ds(first, count), cells, :],
+                    vx.at[0, pl.ds(RIM + j * RUN + first, count), pl.ds(RIM, COLS)],
+                    t_send.at[part, d],
+                    t_recv.at[part, d],
+                    there,
+                )
             )
-        )
-
-    @pl.when(ocean)
-    def _():
-        for copy in index_copies:
-            copy.start()
 
     for copy in state_copies:
         copy.start()
-    nidx[j] = idq[q]
+
+    @pl.when(ocean)
+    def _():
+        for copy in rest_copies + index_copies:
+            copy.start()
+        nidx[j] = idq[q]
+
     for r in range(RUN):
         piece = vt[r, pl.ds(pl.multiple_of(q * COLS, COLS), COLS), :]
         vx[0, RIM + j * RUN + r, RIM : RIM + COLS, :] = piece
 
-    def halo_copies(i):
-        rows = pl.ds(RIM + RUN * i, RUN)
+    def halo_copies(i, rest=0, kinds=range(5)):
+        first_row = RUN * i + (3 if rest else 0)
+        rows = pl.ds(RIM + first_row, 1 if rest else 3)
         up = i < 2
         zone = jnp.where(up, z_up, z_down)
-        landing = pl.ds(jnp.where(up, EROWS - RIM + RUN * i, RUN * i - RIM), RUN)
+        landing = jnp.where(up, EROWS - RIM + first_row, first_row - RIM)
+        landing = pl.ds(landing, 1 if rest else 3)
         inner, first, end = pl.ds(RIM, COLS), pl.ds(RIM, RIM), pl.ds(COLS, RIM)
         before, after = pl.ds(0, RIM), pl.ds(RIM + COLS, RIM)
         here = vx.at[0]
@@ -274,21 +304,39 @@
             (here.at[rows, end], here.at[rows, before], at(grp, z, r_j, r_s)),
         ]
         return [
-            remote(source, target, h_send.at[kind, i], h_recv.at[kind, i], device)
+            remote(source, target, h_send.at[rest, kind, i], h_recv.at[rest, kind, i], device)
             for kind, (source, target, device) in enumerate(routes)
+            if kind in kinds
         ]
 
-    for copy in halo_copies(j):
-        copy.start()
-
-    loads[2].wait()
+    def send_halo(i):
+        for copy in halo_copies(i):
+            copy.start()
+
+        @pl.when(ocean)
+        def _():
+            for copy in halo_copies(i, 1):
+                copy.start()
+
+    def await_halo(i, kinds):
+        for copy in halo_copies(i, 0, kinds):
+            copy.wait_recv()
+
+        @pl.when(ocean)
+        def _():
+            for copy in halo_copies(i, 1, kinds):
+                copy.wait_recv()
+
+    send_halo(j)
+
+    loads[1].wait()
     used = jnp.logical_or(iota((LEV, LEV), 0) < LA, ocean)
     m_high, m_low = pieces(jnp.where(used, jnp.transpose(mixing[...]), 0.0))
     for a in range(2):
         w2[a * LEV : (a + 1) * LEV, 0:LEV] = m_high
         w2[a * LEV : (a + 1) * LEV, LEV : 2 * LEV] = m_low
 
-    loads[7].wait()
+    loads[6].wait()
     place = src[...]
     owner = (place // CELLS) * RUN + (place % BS) // COLS
     inside = ((place % CELLS) // BS) * COLS + place % COLS
@@ -301,11 +349,15 @@
         spot = slice(first * ECOLS, (first + 2) * ECOLS)
         sp[slot, spot, :] = jnp.zeros((2 * ECOLS, 2 * LEV), BF16)
 
-    loads[3].wait()
+    loads[2].wait()
     for d in range(1, RUN):
         state_copies[d - 1].wait_recv()
-        for copy in halo_copies(run_peers[d]):
-            copy.start()
+
+        @pl.when(ocean)
+        def _(d=d):
+            rest_copies[d - 1].wait_recv()
+
+        send_halo(run_peers[d])
 
     gap = iota((BLOCK, BAND), 1) - iota((BLOCK, BAND), 0) - 2 * ECOLS
     gap = gap.astype(F32)
@@ -333,22 +385,42 @@
 
         lax.fori_loop(0, 7, one, 0)
 
+    def count_blocks(first, end):
+        @pl.when(atmos)
+        def _():
+            def one(b, carry):
+                count(b, vx[0, pl.ds(4 * b + 2, 4)].reshape(BLOCK, LEV), TAG)
+                return carry
+
+            lax.fori_loop(first, end, one, 0)
+
+    def unpack(first, end):
+        @pl.when(atmos)
+        def _():
+            for g in range(first, end):
+                fourth = lane_roll(vx[0, 4 * g], THIRD)
+                for r in range(1, 3):
+                    moved = lane_roll(vx[0, 4 * g + r], (r + 1) * THIRD + LEV - PACK - THIRD)
+                    fourth = jnp.where(lane < r * THIRD, fourth, moved)
+                vx[0, 4 * g + 3] = fourth
+
+        for g in range(first, end):
+            high, low = pieces(vx[0, 4 * g : 4 * g + 4].reshape(BLOCK, LEV))
+            sp[0, 4 * g * ECOLS : (4 * g + 4) * ECOLS, 0:LEV] = high
+            sp[0, 4 * g * ECOLS : (4 * g + 4) * ECOLS, LEV : 2 * LEV] = low
+
     for i in range(RUN):
-        for copy in halo_copies(i):
-            copy.wait_recv()
-
-    @pl.when(atmos)
-    def _():
-        def one(b, carry):
-            count(b, vx[0, pl.ds(4 * b + 2, 4)].reshape(BLOCK, LEV), TAG)
-            return carry
-
-        lax.fori_loop(0, 7, one, 0)
-
-    for row in range(0, EROWS, 4):
-        high, low = pieces(vx[0, row : row + 4].reshape(BLOCK, LEV))
-        sp[0, row * ECOLS : (row + 4) * ECOLS, 0:LEV] = high
-        sp[0, row * ECOLS : (row + 4) * ECOLS, LEV : 2 * LEV] = low
+        await_halo(i, (3, 4))
+    unpack(2, 6)
+    count_blocks(2, 5)
+    for i in (2, 3):
+        await_halo(i, (0, 1, 2))
+    unpack(0, 2)
+    count_blocks(0, 2)
+    for i in (0, 1):
+        await_halo(i, (0, 1, 2))
+    unpack(6, 8)
+    count_blocks(5, 7)
 
     def step(n, blocks):
         for b in blocks:
@@ -392,11 +464,15 @@
             for i in range(RUN)
         ]
 
-    loads[4].wait()
+    loads[3].wait()
 
     @pl.when(atmos)
     def _():
-        flux = exact_dot(rows8(fm[...]), own(1) + own(2) + own(3) + own(4), NT) * (1.0 / STEPS)
+        f_high, f_low = pieces(rows8(fm[...]) * (1.0 / STEPS))
+        v_high, v_low = pieces(own(1) + own(2) + own(3) + own(4))
+        weights = jnp.concatenate([f_high, f_low], axis=0)
+        flux = fast_dot(weights, v_high, NT)
+        flux = flux[0:8] + flux[8:16] + fast_dot(f_high, v_low, NT)
         for i in range(RUN):
             fx[i] = flux[:, i * BS : (i + 1) * BS]
         for i, copy in enumerate(flux_copies(0)):
@@ -432,10 +508,10 @@
         piece = vx[last, RIM + j * RUN + r, RIM : RIM + COLS, :]
         rt[r, pl.ds(pl.multiple_of(q * COLS, COLS), COLS), :] = piece
 
+    loads[4].wait()
     loads[5].wait()
-    loads[6].wait()
+    loads[7].wait()
     loads[8].wait()
-    loads[9].wait()
     to_atmos = remote(bmsg, bin_, b_send, b_recv, at(1 - grp, z, j, s))
     force_t = rows8(force[...])
     pushed_t = force_t + exact_dot(force_t, mixing[...], NT)
@@ -563,6 +639,12 @@
         for copy in halo_copies(i):
             copy.wait_send()
 
+        @pl.when(ocean)
+        def _(i=i):
+            for copy in halo_copies(i, 1):
+                copy.wait_send()
+
+
     @pl.when(atmos)
     def _():
         for i, copy in enumerate(flux_copies(0)):
@@ -577,7 +659,7 @@
     @pl.when(ocean)
     def _():
         to_atmos.wait_send()
-        for copy in index_copies:
+        for copy in index_copies + rest_copies:
             copy.wait_send()
 
 
@@ -626,11 +708,11 @@
         vmem((8, CELLS + BS), F32),
         vmem((n_sub, ROWS, BS), F32),
         vmem((n_sub, ROWS, BS), F32),
-        dma((10,)),
-        dma((2, RUN)),
-        dma((2, RUN)),
-        dma((5, RUN)),
-        dma((5, RUN)),
+        dma((9 + RUN,)),
+        dma((3, RUN)),
+        dma((3, RUN)),
+        dma((2, 5, RUN)),
+        dma((2, 5, RUN)),
         dma((2, RUN)),
         dma((RUN,)),
         dma((RUN,)),

time: 61 us -> 60.1 us (0.985); the launches traced: 60.8 us -> 59.2 us
  Pallas kernels: 58.9 us -> 57.2 us
    pallas_call x1, Pallas kernels: 58.9 us -> 57.2 us  [local(): pl.pallas_call(kernel, name='window', out_shape=(jax.ShapeDtypeStruct((1,...]
where the time goes in v3:
time: 60.1 us; the launch traced here: 59.2 us
  Pallas kernels  57.2 us (95%)
  local copies, waits for them, and re-layouts  1.3 us (2%)
  between operations  0.64 us (1%)
    pallas_call x1, Pallas kernels, local(): pl.pallas_call(kernel, name='window', out_shape=(jax.ShapeDtypeStruct((1,...  57.2 us
    unnamed x2, local copies, waits for them, and re-layouts  1.3 us

profile of v3, /device:TPU:1, one launch (start us, length us, event | category | flops | bytes accessed | tf_op | source)
XLA Modules:
  0.0 59.2 jit_solution(18231190540469657566)
XLA Ops:
  0.6 57.2 %window.1 = (f32[1,128,512]{2,1,0:T(8,128)S(1)}, f32[3,512]{1,0:T(4,128)S(1)}) custom-call(f32[1,128,512]{2,1,0:T(8,128)} %refs_0_.1, s32[3,1,512]{2,1,0:T(1,128)} %bitcast.3, f32[1,128,128]{2,1,0:T(8,128)} %refs_2_.1, f32[1,128]{1,0:T(1,128)} %refs_3_.1, f32[4,128]{1,0:T(4,128)} %refs_4_.1, f32[4,128]{1,0:T(4,128)} %bitcast.4, f32[3,128]{1,0:T(4,128)} %refs_6_.1, ...), custom_call_target="tpu_custom_call" | custom-call | tf_op jit(solution)/shard_map/window/pallas_call | solution.py:729
  57.9 0.7 %copy.14 = f32[1,128,512]{2,1,0:T(8,128)} copy(f32[1,128,512]{2,1,0:T(8,128)S(1)} %get-tuple-element.4) | data formatting | bytes 524288
  58.6 0.6 %copy.15 = f32[3,512]{1,0:T(4,128)} copy(f32[3,512]{1,0:T(4,128)S(1)} %get-tuple-element.5) | data formatting | bytes 12288

commit v4 on v3

--- a/solution.py
+++ b/solution.py
@@ -110,8 +110,10 @@
     ft,
     ftab,
     rt,
-    bmsg,
+    bx,
     bin_,
+    gx,
+    gin,
     pbuf,
     cin,
     in_sem,
@@ -127,6 +129,8 @@
     x_recv,
     b_send,
     b_recv,
+    g_send,
+    g_recv,
 ):
     grp = lax.axis_index("grp")
     reg = lax.axis_index("reg")
@@ -452,17 +456,24 @@
     def own(n):
         return vx[n, RIM : RIM + ROWS, RIM : RIM + COLS, :].reshape(CELLS, LEV)
 
-    def flux_copies(g):
+    def to_owners(g, source, target, send, recv):
         return [
-            remote(
-                fx.at[i],
-                fin.at[q],
-                f_send.at[g, i],
-                f_recv.at[j],
-                at(g, z, i, s),
-            )
+            remote(source.at[i], target.at[q], send.at[g, i], recv.at[j], at(g, z, i, s))
             for i in range(RUN)
         ]
+
+    def flux_copies(g):
+        return to_owners(g, fx, fin, f_send, f_recv)
+
+    def base_copies(g):
+        return to_owners(g, bx, bin_, b_send, b_recv)
+
+    def but_own(copies, act):
+        for i, copy in enumerate(copies):
+
+            @pl.when(j != i)
+            def _(copy=copy):
+                act(copy)
 
     loads[3].wait()
 
@@ -475,14 +486,9 @@
         flux = flux[0:8] + flux[8:16] + fast_dot(f_high, v_low, NT)
         for i in range(RUN):
             fx[i] = flux[:, i * BS : (i + 1) * BS]
-        for i, copy in enumerate(flux_copies(0)):
-
-            @pl.when(j != i)
-            def _(copy=copy):
-                copy.start()
-
         for copy in flux_copies(1):
             copy.start()
+        but_own(flux_copies(0), lambda copy: copy.start())
         fin[q] = fx[j]
 
     last = n_steps
@@ -499,38 +505,35 @@
             )
         )
 
-    @pl.when(ocean)
-    def _():
-        for copy in back_copies:
-            copy.start()
-
-    for r in range(RUN):
-        piece = vx[last, RIM + j * RUN + r, RIM : RIM + COLS, :]
-        rt[r, pl.ds(pl.multiple_of(q * COLS, COLS), COLS), :] = piece
-
     loads[4].wait()
     loads[5].wait()
     loads[7].wait()
     loads[8].wait()
-    to_atmos = remote(bmsg, bin_, b_send, b_recv, at(1 - grp, z, j, s))
+    to_atmos = remote(gx, gin, g_send, g_recv, at(1 - grp, z, j, s))
     force_t = rows8(force[...])
     pushed_t = force_t + exact_dot(force_t, mixing[...], NT)
 
     @pl.when(ocean)
     def _():
-        for copy in back_copies:
-            copy.wait_recv()
         returns = rows8(rm[...])
-        base = exact_dot(returns, rt[...].reshape(CELLS, LEV), NT)
+        base = exact_dot(returns, own(1), NT)
+        for i in range(RUN):
+            bx[i] = base[:, i * BS : (i + 1) * BS]
+        for copy in base_copies(0):
+            copy.start()
+        but_own(base_copies(1), lambda copy: copy.start())
+        bin_[q] = bx[j]
         gains = jnp.zeros((8, BS), F32)
         for f in range(4):
             gain = jnp.sum(returns * pushed_t[f : f + 1, :], axis=1, keepdims=True)
             gains = jnp.where(iota((8, BS), 1) == f, gain, gains)
-        bmsg[:, 0:CELLS] = base
-        bmsg[:, CELLS : CELLS + BS] = gains
-        bin_[:, 0:CELLS] = base
-        bin_[:, CELLS : CELLS + BS] = gains
+        gx[...] = gains
+        gin[...] = gains
         to_atmos.start()
+
+    for r in range(RUN):
+        piece = vx[last, RIM + j * RUN + r, RIM : RIM + COLS, :]
+        rt[r, pl.ds(pl.multiple_of(q * COLS, COLS), COLS), :] = piece
 
     for i in range(RUN):
 
@@ -558,10 +561,22 @@
     for copy in gather_copies:
         copy.start()
 
+    for copy in back_copies:
+        copy.start()
+
+    for i in range(RUN):
+
+        @pl.when(jnp.logical_or(atmos, j != i))
+        def _(i=i):
+            device = at(1 - grp, z, i, s)
+            remote(bx.at[i], bin_.at[i], b_send.at[0, i], b_recv.at[i], device).wait_recv()
+
     @pl.when(atmos)
     def _():
-        for copy in back_copies:
-            copy.start()
+        to_atmos.wait_recv()
+
+    base = regroup([bin_[c] for c in range(RUN)], RUN)
+    base = jnp.concatenate(base, axis=1)
 
     for copy in gather_copies:
         copy.wait_recv()
@@ -578,15 +593,10 @@
         ocean_flux = ocean_flux + rw[k : k + 1, :] * taken
     ocean_flux = ocean_flux + pltpu.roll(ocean_flux, 4, 0)
 
-    @pl.when(atmos)
-    def _():
-        to_atmos.wait_recv()
-
     wet_f = wet[...].astype(F32)
-    surface = bin_[:, 0:CELLS]
+    surface = base
     for f in range(4):
-        gain = bin_[:, CELLS + f : CELLS + f + 1]
-        surface = surface + gain * ocean_flux[f : f + 1, :]
+        surface = surface + gin[:, f : f + 1] * ocean_flux[f : f + 1, :]
     surface = surface * wet_f
     surface = surface + pltpu.roll(surface, 4, 0)
     sums = None
@@ -608,10 +618,11 @@
         copy.start()
     cin[s] = pbuf[s]
 
+    for copy in back_copies:
+        copy.wait_recv()
+
     @pl.when(atmos)
     def _():
-        for copy in back_copies:
-            copy.wait_recv()
         for r in range(RUN):
             ns_out[0, :, r * BS : (r + 1) * BS] = jnp.transpose(rt[r])
 
@@ -647,18 +658,16 @@
 
     @pl.when(atmos)
     def _():
-        for i, copy in enumerate(flux_copies(0)):
-
-            @pl.when(j != i)
-            def _(copy=copy):
-                copy.wait_send()
-
+        but_own(flux_copies(0), lambda copy: copy.wait_send())
         for copy in flux_copies(1):
             copy.wait_send()
 
     @pl.when(ocean)
     def _():
         to_atmos.wait_send()
+        but_own(base_copies(1), lambda copy: copy.wait_send())
+        for copy in base_copies(0):
+            copy.wait_send()
         for copy in index_copies + rest_copies:
             copy.wait_send()
 
@@ -704,8 +713,10 @@
         vmem((ROWS, BS), F32),
         vmem((n_sub, ROWS, BS), F32),
         vmem((RUN, BS, LEV), F32),
-        vmem((8, CELLS + BS), F32),
-        vmem((8, CELLS + BS), F32),
+        vmem((RUN, 8, BS), F32),
+        vmem((RUN, 8, BS), F32),
+        vmem((8, BS), F32),
+        vmem((8, BS), F32),
         vmem((n_sub, ROWS, BS), F32),
         vmem((n_sub, ROWS, BS), F32),
         dma((9 + RUN,)),
@@ -719,6 +730,8 @@
         dma((RUN,)),
         dma((2, n_sub)),
         dma((2, n_sub)),
+        dma((2, RUN)),
+        dma((RUN,)),
         dma(()),
         dma(()),
     ]

time: 60.1 us -> 59.4 us (0.988); the launches traced: 59.2 us -> 59.2 us
  no operation moved by 1% of the time
where the time goes in v4:
time: 59.4 us; the launch traced here: 59.2 us
  Pallas kernels  57.3 us (96%)
  local copies, waits for them, and re-layouts  1.3 us (2%)
  between operations  0.64 us (1%)
    pallas_call x1, Pallas kernels, local(): pl.pallas_call(kernel, name='window', out_shape=(jax.ShapeDtypeStruct((1,...  57.3 us
    unnamed x2, local copies, waits for them, and re-layouts  1.3 us

profile of v4, /device:TPU:1, one launch (start us, length us, event | category | flops | bytes accessed | tf_op | source)
XLA Modules:
  0.0 59.2 jit_solution(2300954927993866589)
XLA Ops:
  0.6 57.3 %window.1 = (f32[1,128,512]{2,1,0:T(8,128)S(1)}, f32[3,512]{1,0:T(4,128)S(1)}) custom-call(f32[1,128,512]{2,1,0:T(8,128)} %refs_0_.1, s32[3,1,512]{2,1,0:T(1,128)} %bitcast.3, f32[1,128,128]{2,1,0:T(8,128)} %refs_2_.1, f32[1,128]{1,0:T(1,128)} %refs_3_.1, f32[4,128]{1,0:T(4,128)} %refs_4_.1, f32[4,128]{1,0:T(4,128)} %bitcast.4, f32[3,128]{1,0:T(4,128)} %refs_6_.1, ...), custom_call_target="tpu_custom_call" | custom-call | tf_op jit(solution)/shard_map/window/pallas_call | solution.py:742
  57.9 0.7 %copy.14 = f32[1,128,512]{2,1,0:T(8,128)} copy(f32[1,128,512]{2,1,0:T(8,128)S(1)} %get-tuple-element.4) | data formatting | bytes 524288
  58.6 0.6 %copy.15 = f32[3,512]{1,0:T(4,128)} copy(f32[3,512]{1,0:T(4,128)S(1)} %get-tuple-element.5) | data formatting | bytes 12288

commit v5 on v4

--- a/solution.py
+++ b/solution.py
@@ -207,7 +207,6 @@
         load.start()
 
     lane = iota((1, LEV), 1)
-    keep = jnp.logical_or(lane < LA, ocean).astype(F32)
     loads[0].wait()
     link = rows8(jnp.concatenate([nb[k] for k in range(3)], axis=0))
     e_row = jnp.zeros_like(link)
@@ -334,7 +333,8 @@
     send_halo(j)
 
     loads[1].wait()
-    used = jnp.logical_or(iota((LEV, LEV), 0) < LA, ocean)
+    used = jnp.maximum(iota((LEV, LEV), 0), iota((LEV, LEV), 1)) < LA
+    used = jnp.logical_or(used, ocean)
     m_high, m_low = pieces(jnp.where(used, jnp.transpose(mixing[...]), 0.0))
     for a in range(2):
         w2[a * LEV : (a + 1) * LEV, 0:LEV] = m_high
@@ -426,32 +426,37 @@
     unpack(6, 8)
     count_blocks(5, 7)
 
-    def step(n, blocks):
-        for b in blocks:
-            row = 4 * b + 2
-            acc = fast_dot(cnt[b], sp[n, 4 * b * ECOLS : 4 * b * ECOLS + BAND, :], NN)
-            field = vx[n, row : row + 4].reshape(BLOCK, LEV)
-            total = acc[:, 0:LEV] + acc[:, LEV : 2 * LEV]
-            spread = field + rate[...] * (total - 3.0 * field)
+    stay = 1.0 - 3.0 * rate[...]
+
+    def step(n, halves):
+        for b in range(7):
+            mine = [h for h in (0, 1) if 2 * b + h in halves]
+            if not mine:
+                continue
+            height = 2 * len(mine)
+            cells = height * ECOLS
+            shift = 2 * mine[0]
+            row = 4 * b + 2 + shift
+            counts = cnt[b, shift * ECOLS : shift * ECOLS + cells, :]
+            acc = fast_dot(counts, sp[n, 4 * b * ECOLS : 4 * b * ECOLS + BAND, :], NN)
+            field = vx[n, row : row + height].reshape(cells, LEV)
+            spread = stay * field + rate[...] * (acc[:, 0:LEV] + acc[:, LEV : 2 * LEV])
             high, low = pieces(spread)
             mixed = fast_dot(jnp.concatenate([high, low], axis=1), w2[...], NN)
-            new = keep * (spread + mixed[:, 0:LEV] + mixed[:, LEV : 2 * LEV])
-            vx[n + 1, row : row + 4] = new.reshape(4, ECOLS, LEV)
-            high, low = pieces(new)
-            sp[n + 1, row * ECOLS : row * ECOLS + BLOCK, 0:LEV] = high
-            sp[n + 1, row * ECOLS : row * ECOLS + BLOCK, LEV : 2 * LEV] = low
-
-    def wide(n, carry):
-        step(n, range(7))
-        return carry
-
-    def narrow(n, carry):
-        step(n, range(1, 6))
-        return carry
+            new = spread + (mixed[:, 0:LEV] + mixed[:, LEV : 2 * LEV])
+            vx[n + 1, row : row + height] = new.reshape(height, ECOLS, LEV)
+            if n < STEPS - 1:
+                high, low = pieces(new)
+                sp[n + 1, row * ECOLS : row * ECOLS + cells, 0:LEV] = high
+                sp[n + 1, row * ECOLS : row * ECOLS + cells, LEV : 2 * LEV] = low
 
     n_steps = jnp.where(ocean, 1, STEPS)
-    lax.fori_loop(0, jnp.where(ocean, 1, 2), wide, 0)
-    lax.fori_loop(jnp.where(ocean, STEPS, 2), STEPS, narrow, 0)
+    step(0, range(14))
+
+    @pl.when(atmos)
+    def _():
+        for n in range(1, STEPS):
+            step(n, range(n, 14 - n))
 
     def own(n):
         return vx[n, RIM : RIM + ROWS, RIM : RIM + COLS, :].reshape(CELLS, LEV)
@@ -474,22 +479,6 @@
             @pl.when(j != i)
             def _(copy=copy):
                 act(copy)
-
-    loads[3].wait()
-
-    @pl.when(atmos)
-    def _():
-        f_high, f_low = pieces(rows8(fm[...]) * (1.0 / STEPS))
-        v_high, v_low = pieces(own(1) + own(2) + own(3) + own(4))
-        weights = jnp.concatenate([f_high, f_low], axis=0)
-        flux = fast_dot(weights, v_high, NT)
-        flux = flux[0:8] + flux[8:16] + fast_dot(f_high, v_low, NT)
-        for i in range(RUN):
-            fx[i] = flux[:, i * BS : (i + 1) * BS]
-        for copy in flux_copies(1):
-            copy.start()
-        but_own(flux_copies(0), lambda copy: copy.start())
-        fin[q] = fx[j]
 
     last = n_steps
     back_copies = []
@@ -505,6 +494,24 @@
             )
         )
 
+    loads[3].wait()
+
+    @pl.when(atmos)
+    def _():
+        f_high, f_low = pieces(jnp.where(lane < LA, rows8(fm[...]) * (1.0 / STEPS), 0.0))
+        v_high, v_low = pieces(own(1) + own(2) + own(3) + own(4))
+        weights = jnp.concatenate([f_high, f_low], axis=0)
+        flux = fast_dot(weights, v_high, NT)
+        flux = flux[0:8] + flux[8:16] + fast_dot(f_high, v_low, NT)
+        for i in range(RUN):
+            fx[i] = flux[:, i * BS : (i + 1) * BS]
+        for copy in flux_copies(1):
+            copy.start()
+        but_own(flux_copies(0), lambda copy: copy.start())
+        fin[q] = fx[j]
+        for copy in back_copies:
+            copy.start()
+
     loads[4].wait()
     loads[5].wait()
     loads[7].wait()
@@ -523,6 +530,8 @@
             copy.start()
         but_own(base_copies(1), lambda copy: copy.start())
         bin_[q] = bx[j]
+        for copy in back_copies:
+            copy.start()
         gains = jnp.zeros((8, BS), F32)
         for f in range(4):
             gain = jnp.sum(returns * pushed_t[f : f + 1, :], axis=1, keepdims=True)
@@ -559,9 +568,6 @@
 
     gather_copies = over_sub(lambda peer: ft, ftab, 0)
     for copy in gather_copies:
-        copy.start()
-
-    for copy in back_copies:
         copy.start()
 
     for i in range(RUN):
@@ -624,7 +630,8 @@
     @pl.when(atmos)
     def _():
         for r in range(RUN):
-            ns_out[0, :, r * BS : (r + 1) * BS] = jnp.transpose(rt[r])
+            block = jnp.transpose(rt[r])
+            ns_out[0, :, r * BS : (r + 1) * BS] = jnp.where(iota((LEV, BS), 0) < LA, block, 0.0)
 
     @pl.when(ocean)
     def _():

time: 59.4 us -> 60.2 us (1.013)
  Pallas kernels: 57.3 us -> 58.1 us
    pallas_call x1, Pallas kernels: 57.3 us -> 58.1 us  [local(): pl.pallas_call(kernel, name='window', out_shape=(jax.ShapeDtypeStruct((1,...]
where the time goes in v5:
time: 60.2 us; the launch traced here: 60 us
  Pallas kernels  58.1 us (97%)
  local copies, waits for them, and re-layouts  1.3 us (2%)
  between operations  0.64 us (1%)
    pallas_call x1, Pallas kernels, local(): pl.pallas_call(kernel, name='window', out_shape=(jax.ShapeDtypeStruct((1,...  58.1 us
    unnamed x2, local copies, waits for them, and re-layouts  1.3 us

profile of v5, /device:TPU:1, one launch (start us, length us, event | category | flops | bytes accessed | tf_op | source)
XLA Modules:
  0.0 60.0 jit_solution(12159914772189273465)
XLA Ops:
  0.6 58.1 %window.1 = (f32[1,128,512]{2,1,0:T(8,128)S(1)}, f32[3,512]{1,0:T(4,128)S(1)}) custom-call(f32[1,128,512]{2,1,0:T(8,128)} %refs_0_.1, s32[3,1,512]{2,1,0:T(1,128)} %bitcast.3, f32[1,128,128]{2,1,0:T(8,128)} %refs_2_.1, f32[1,128]{1,0:T(1,128)} %refs_3_.1, f32[4,128]{1,0:T(4,128)} %refs_4_.1, f32[4,128]{1,0:T(4,128)} %bitcast.4, f32[3,128]{1,0:T(4,128)} %refs_6_.1, ...), custom_call_target="tpu_custom_call" | custom-call | tf_op jit(solution)/shard_map/window/pallas_call | solution.py:749
  58.7 0.7 %copy.14 = f32[1,128,512]{2,1,0:T(8,128)} copy(f32[1,128,512]{2,1,0:T(8,128)S(1)} %get-tuple-element.4) | data formatting | bytes 524288
  59.4 0.6 copy.15

commit v6 on v5

--- a/solution.py
+++ b/solution.py
@@ -481,18 +481,20 @@
                 act(copy)
 
     last = n_steps
-    back_copies = []
+    back_copies, back_rest = [], []
     for d in range(1, RUN):
         peer = run_peers[d]
-        back_copies.append(
-            remote(
-                vx.at[last, pl.ds(RIM + peer * RUN, RUN), pl.ds(RIM, COLS)],
-                rt.at[:, pl.ds(pl.multiple_of(q * COLS, COLS), COLS), :],
-                r_send.at[d],
-                r_recv.at[d],
-                at(grp, z, peer, s),
+        cells = pl.ds(pl.multiple_of(q * COLS, COLS), COLS)
+        for part, copies, first, count_of in ((0, back_copies, 0, 3), (1, back_rest, 3, 1)):
+            copies.append(
+                remote(
+                    vx.at[last, pl.ds(RIM + peer * RUN + first, count_of), pl.ds(RIM, COLS)],
+                    rt.at[pl.ds(first, count_of), cells, :],
+                    r_send.at[part, d],
+                    r_recv.at[part, d],
+                    at(grp, z, peer, s),
+                )
             )
-        )
 
     loads[3].wait()
 
@@ -509,8 +511,12 @@
             copy.start()
         but_own(flux_copies(0), lambda copy: copy.start())
         fin[q] = fx[j]
-        for copy in back_copies:
-            copy.start()
+        for g in range(RUN):
+            fourth = vx[STEPS, RIM + 4 * g + 3, RIM : RIM + COLS, :]
+            for r in range(3):
+                kept = vx[STEPS, RIM + 4 * g + r, RIM : RIM + COLS, :]
+                kept = jnp.where(lane < PACK, kept, lane_roll(fourth, PACK - r * THIRD))
+                vx[STEPS, RIM + 4 * g + r, RIM : RIM + COLS, :] = kept
 
     loads[4].wait()
     loads[5].wait()
@@ -530,7 +536,7 @@
             copy.start()
         but_own(base_copies(1), lambda copy: copy.start())
         bin_[q] = bx[j]
-        for copy in back_copies:
+        for copy in back_copies + back_rest:
             copy.start()
         gains = jnp.zeros((8, BS), F32)
         for f in range(4):
@@ -569,6 +575,11 @@
     gather_copies = over_sub(lambda peer: ft, ftab, 0)
     for copy in gather_copies:
         copy.start()
+
+    @pl.when(atmos)
+    def _():
+        for copy in back_copies:
+            copy.start()
 
     for i in range(RUN):
 
@@ -624,17 +635,30 @@
         copy.start()
     cin[s] = pbuf[s]
 
+    for copy in sum_copies:
+        copy.wait_recv()
+    summed = cin[...].sum(axis=0)
+    by_chunk = [rows8(summed[c * 4 : (c + 1) * 4, :]) for c in range(RUN)]
+    for r, block in enumerate(regroup(by_chunk, RUN)):
+        cpl_out[:, r * BS : (r + 1) * BS] = block[0:3, :]
+
     for copy in back_copies:
         copy.wait_recv()
 
     @pl.when(atmos)
     def _():
+        fourth = lane_roll(rt[0], THIRD)
+        for r in range(1, 3):
+            fourth = jnp.where(lane < r * THIRD, fourth, lane_roll(rt[r], (r + 1) * THIRD))
+        rt[3] = fourth
         for r in range(RUN):
             block = jnp.transpose(rt[r])
             ns_out[0, :, r * BS : (r + 1) * BS] = jnp.where(iota((LEV, BS), 0) < LA, block, 0.0)
 
     @pl.when(ocean)
     def _():
+        for copy in back_rest:
+            copy.wait_recv()
         columns = jnp.transpose(jnp.concatenate([pushed_t, jnp.zeros((BS - 8, BS), F32)], axis=0))
         for r in range(RUN):
             part = slice(r * BS, (r + 1) * BS)
@@ -644,13 +668,6 @@
             old = start[:, part]
             ns_out[0, :, part] = old + wet_f[:, part] * (forced - old)
 
-    for copy in sum_copies:
-        copy.wait_recv()
-    summed = cin[...].sum(axis=0)
-    by_chunk = [rows8(summed[c * 4 : (c + 1) * 4, :]) for c in range(RUN)]
-    for r, block in enumerate(regroup(by_chunk, RUN)):
-        cpl_out[:, r * BS : (r + 1) * BS] = block[0:3, :]
-
     for copy in state_copies + back_copies + gather_copies + sum_copies:
         copy.wait_send()
     for i in range(RUN):
@@ -675,7 +692,7 @@
         but_own(base_copies(1), lambda copy: copy.wait_send())
         for copy in base_copies(0):
             copy.wait_send()
-        for copy in index_copies + rest_copies:
+        for copy in index_copies + rest_copies + back_rest:
             copy.wait_send()
 
 
@@ -733,8 +750,8 @@
         dma((2, 5, RUN)),
         dma((2, RUN)),
         dma((RUN,)),
-        dma((RUN,)),
-        dma((RUN,)),
+        dma((2, RUN)),
+        dma((2, RUN)),
         dma((2, n_sub)),
         dma((2, n_sub)),
         dma((2, RUN)),

time: 60.2 us -> 59 us (0.980)
  Pallas kernels: 58.1 us -> 56.9 us
    pallas_call x1, Pallas kernels: 58.1 us -> 56.9 us  [local(): pl.pallas_call(kernel, name='window', out_shape=(jax.ShapeDtypeStruct((1,...]
where the time goes in v6:
time: 59 us; the launch traced here: 58.8 us
  Pallas kernels  56.9 us (96%)
  local copies, waits for them, and re-layouts  1.3 us (2%)
  between operations  0.64 us (1%)
    pallas_call x1, Pallas kernels, local(): pl.pallas_call(kernel, name='window', out_shape=(jax.ShapeDtypeStruct((1,...  56.9 us
    unnamed x2, local copies, waits for them, and re-layouts  1.3 us

profile of v6, /device:TPU:1, one launch (start us, length us, event | category | flops | bytes accessed | tf_op | source)
XLA Modules:
  0.0 58.8 jit_solution(16484160694311726021)
XLA Ops:
  0.6 56.9 %window.1 = (f32[1,128,512]{2,1,0:T(8,128)S(1)}, f32[3,512]{1,0:T(4,128)S(1)}) custom-call(f32[1,128,512]{2,1,0:T(8,128)} %refs_0_.1, s32[3,1,512]{2,1,0:T(1,128)} %bitcast.3, f32[1,128,128]{2,1,0:T(8,128)} %refs_2_.1, f32[1,128]{1,0:T(1,128)} %refs_3_.1, f32[4,128]{1,0:T(4,128)} %refs_4_.1, f32[4,128]{1,0:T(4,128)} %bitcast.4, f32[3,128]{1,0:T(4,128)} %refs_6_.1, ...), custom_call_target="tpu_custom_call" | custom-call | tf_op jit(solution)/shard_map/window/pallas_call | solution.py:766
  57.5 0.7 %copy.14 = f32[1,128,512]{2,1,0:T(8,128)} copy(f32[1,128,512]{2,1,0:T(8,128)S(1)} %get-tuple-element.4) | data formatting | bytes 524288
  58.2 0.6 %copy.15 = f32[3,512]{1,0:T(4,128)} copy(f32[3,512]{1,0:T(4,128)S(1)} %get-tuple-element.5) | data formatting | bytes 12288
